TPU v7x, 256 devices: a whole 4x4x8 slice. The times are simulated.
256 devices in a mesh: seq: 32 (over y, z), dp: 2 (over core), head: 4 (over x).
Axes of the slice: x: 4, y: 4, z: 8, core: 2. Of those that a mesh axis runs over, the one named last changes fastest.
Arguments:
- inputs: bfloat16 [2, 12288, 3072], P('dp', 'seq'), may hold values from -40 to 40
- w_query: bfloat16 [3072, 2048], P(None, 'head'), may hold values from -0.21650635 to 0.21650635
- w_key: bfloat16 [3072, 2048], P(None, 'head'), may hold values from -0.07216878 to 0.07216878
- w_value: bfloat16 [3072, 2048], P(None, 'head'), may hold values from -0.108253175 to 0.108253175
- gate_bias: float32 [8], P('head'), may hold values from 0 to 2.5
- cotangent: bfloat16 [2, 12288, 2048], P('dp', 'seq', 'head'), may hold values from -8 to 8
Outputs:
- blended: bfloat16 [2, 12288, 2048], P('dp', 'seq', 'head')
- grad_weights: float32 [3072, 3, 2048], P(('seq', 'dp'), None, 'head')
All inputs are finite; a program needn't handle non-finite values.
Results may differ from a plain program's by a relative error of at most 0.012.
Values may be sent and summed in bfloat16 or wider, within the bound.
A program may use at most 128 MiB of HBM per device.

v0:
```python
import math

import jax
import jax.numpy as jnp
from jax import lax
from jax.sharding import Mesh
from jax.sharding import PartitionSpec as P

SEQ = ("seq_0", "seq_1")
SEQ_DP = ("seq_0", "seq_1", "dp")


def filled_with(x, identity):
    return jax.tree.map(
        lambda a, e: jnp.broadcast_to(jnp.asarray(e, a.dtype), a.shape), x, identity
    )


def prefix_by_axis(x, axes, combine, identity, reverse):
    before = start = filled_with(x, identity)
    subtotal = x
    for axis in reversed(axes):
        devices, position = (lax.axis_size(axis), lax.axis_index(axis))
        pieces = jax.tree.map(lambda part: lax.all_gather(part, axis), subtotal)
        inside, subtotal = (start, start)
        for k in reversed(range(devices)) if reverse else range(devices):
            passed = k > position if reverse else k < position
            subtotal = combine(subtotal, jax.tree.map(lambda part: part[k], pieces))
            inside = jax.tree.map(lambda new, old: jnp.where(passed, new, old), subtotal, inside)
        before = combine(inside, before)
    return before


def passed_along(x, axis, by):
    devices = lax.axis_size(axis)
    pairs = [(i, i + by) for i in range(devices) if 0 <= i + by < devices]
    return lax.ppermute(x, axis, pairs)


def product(form, left, right):
    return jnp.einsum(form, left, right, preferred_element_type=jnp.float32)


def feature(values_in):
    return jnp.where(values_in > 0, values_in + 1.0, jnp.exp(jnp.minimum(values_in, 0.0)))


def feature_slope(values_in):
    return jnp.where(values_in > 0, 1.0, jnp.exp(jnp.minimum(values_in, 0.0)))


def add_pair(earlier, latter):
    return (earlier[0] + latter[0], earlier[1] + latter[1])


def write_memory(keys_own, values_own):
    phi_key = feature(keys_own.astype(jnp.float32))
    memory = jnp.einsum("shd,she->hde", phi_key, values_own.astype(jnp.float32))
    return (memory, jnp.sum(phi_key, axis=0))


def write_grads(keys_own, values_own, grad_memory, grad_norm):
    key_float = keys_own.astype(jnp.float32)
    phi_key = feature(key_float)
    grad_phi = (
        jnp.einsum("hde,she->shd", grad_memory, values_own.astype(jnp.float32)) + grad_norm[None]
    )
    grad_value = jnp.einsum("shd,hde->she", phi_key, grad_memory)
    return (grad_phi * feature_slope(key_float), grad_value)


def attend(
    queries, keys_own, values_own, keys_prev, values_prev, has_prev, memory, normaliser, gate_bias
):
    seg_len, head_count, head_dim = queries.shape
    all_keys = jnp.concatenate([keys_prev, keys_own], 0)
    all_values = jnp.concatenate([values_prev, values_own], 0)
    score_scale = head_dim ** (-0.5)
    scores = product("shd,thd->hst", queries, all_keys) * score_scale
    row_ids = lax.broadcasted_iota(jnp.int32, (seg_len, 2 * seg_len), 0)
    col_ids = lax.broadcasted_iota(jnp.int32, (seg_len, 2 * seg_len), 1)
    allowed = (col_ids <= row_ids + seg_len) & ((col_ids >= seg_len) | has_prev)
    scores = jnp.where(allowed[None], scores, -1e30)
    row_max = jnp.max(scores, axis=2, keepdims=True)
    weights = jnp.exp(scores - row_max)
    softmax = weights / jnp.sum(weights, axis=2, keepdims=True)
    soft_bf = softmax.astype(jnp.bfloat16)
    local_out = product("hst,thd->shd", soft_bf, all_values)
    phi_query = feature(queries.astype(jnp.float32))
    numerator = jnp.einsum("shd,hde->she", phi_query, memory)
    denominator = jnp.einsum("shd,hd->sh", phi_query, normaliser) + 1.0
    retrieved = numerator / denominator[:, :, None]
    mixing = jax.nn.sigmoid(gate_bias)[None, :, None]
    blended = mixing * retrieved + (1.0 - mixing) * local_out
    stored = (all_keys, all_values, softmax, soft_bf, phi_query, retrieved, denominator)
    return (blended.astype(jnp.bfloat16), stored)


def backprop(cotangent, queries, memory, normaliser, gate_bias, stored):
    all_keys, all_values, softmax, soft_bf, phi_query, retrieved, denominator = stored
    head_dim = queries.shape[2]
    mixing = jax.nn.sigmoid(gate_bias)[None, :, None]
    upstream = cotangent.astype(jnp.float32)
    grad_ret = mixing * upstream
    grad_local = ((1.0 - mixing) * upstream).astype(jnp.bfloat16)
    grad_soft = product("shd,thd->hst", grad_local, all_values)
    grad_values = product("hst,shd->thd", soft_bf, grad_local)
    row_dot = jnp.sum(softmax * grad_soft, axis=2, keepdims=True)
    grad_scores = (softmax * (grad_soft - row_dot) * head_dim ** (-0.5)).astype(jnp.bfloat16)
    grad_query = product("hst,thd->shd", grad_scores, all_keys)
    grad_keys = product("hst,shd->thd", grad_scores, queries)
    grad_num = grad_ret / denominator[:, :, None]
    grad_den = -jnp.sum(grad_ret * retrieved, axis=2) / denominator
    grad_phi = (
        jnp.einsum("she,hde->shd", grad_num, memory) + grad_den[:, :, None] * normaliser[None]
    )
    grad_memory = jnp.einsum("shd,she->hde", phi_query, grad_num)
    grad_norm = jnp.einsum("shd,sh->hd", phi_query, grad_den)
    grad_query = grad_query + grad_phi * feature_slope(queries.astype(jnp.float32))
    return (grad_query, grad_keys, grad_values, grad_memory, grad_norm)


def local(inputs, w_query, w_key, w_value, gate_bias, cotangent):
    tokens = inputs[0]
    seg_len, model_dim = tokens.shape
    head_count = gate_bias.shape[0]
    columns = w_query.shape[1]
    head_dim = columns // head_count

    def project(weight):
        return jnp.dot(tokens, weight, preferred_element_type=jnp.float32).astype(jnp.bfloat16)

    query_flat = project(w_query)
    key_flat = project(w_key)
    value_flat = project(w_value)
    queries = query_flat.reshape(seg_len, head_count, head_dim)
    keys_own = key_flat.reshape(seg_len, head_count, head_dim)
    values_own = value_flat.reshape(seg_len, head_count, head_dim)
    memory_own, norm_own = write_memory(keys_own, values_own)
    zero_pair = (jnp.zeros_like(memory_own), jnp.zeros_like(norm_own))
    memory_prev, norm_prev = prefix_by_axis((memory_own, norm_own), SEQ, add_pair, zero_pair, False)
    neighbour = passed_along(jnp.stack([key_flat, value_flat]), SEQ, 1)
    keys_prev = neighbour[0].reshape(seg_len, head_count, head_dim)
    values_prev = neighbour[1].reshape(seg_len, head_count, head_dim)
    has_prev = lax.axis_index(SEQ) > 0
    blended, stored = attend(
        queries,
        keys_own,
        values_own,
        keys_prev,
        values_prev,
        has_prev,
        memory_prev,
        norm_prev,
        gate_bias,
    )
    cot_local = cotangent[0].reshape(seg_len, head_count, head_dim)
    grad_query, grad_keys, grad_values, grad_memory, grad_norm = backprop(
        cot_local, queries, memory_prev, norm_prev, gate_bias, stored
    )
    grad_mem_seg, grad_norm_seg = prefix_by_axis(
        (grad_memory, grad_norm), SEQ, add_pair, zero_pair, True
    )
    outgoing = jnp.stack([grad_keys[:seg_len], grad_values[:seg_len]]).astype(jnp.bfloat16)
    incoming = passed_along(outgoing, SEQ, -1).astype(jnp.float32)
    write_key, write_value = write_grads(keys_own, values_own, grad_mem_seg, grad_norm_seg)
    grad_key = (grad_keys[seg_len:] + incoming[0] + write_key).astype(jnp.bfloat16)
    grad_value = (grad_values[seg_len:] + incoming[1] + write_value).astype(jnp.bfloat16)
    grad_all = jnp.concatenate(
        [
            grad_query.astype(jnp.bfloat16).reshape(seg_len, columns),
            grad_key.reshape(seg_len, columns),
            grad_value.reshape(seg_len, columns),
        ],
        1,
    )
    seq_count = lax.axis_size(SEQ)
    dp_count = lax.axis_size("dp")
    grad_scale = 1.0 / math.sqrt(seq_count * dp_count * seg_len)
    part_rows = model_dim // (seq_count * dp_count)
    contract = (((0,), (0,)), ((), ()))
    summed = lax.psum_scatter(
        lax.dot_general(tokens, grad_all, contract, preferred_element_type=jnp.float32)
        * grad_scale,
        SEQ_DP,
        scatter_dimension=0,
        tiled=True,
    )
    grad_weights = summed.reshape(part_rows, 3, columns)
    return (blended.reshape(1, seg_len, columns), grad_weights)


def solution(mesh):
    finer = Mesh(
        mesh.devices.reshape(4, 8, mesh.shape["dp"], mesh.shape["head"]),
        ("seq_0", "seq_1", "dp", "head"),
    )
    placed = (
        P("dp", SEQ, None),
        P(None, "head"),
        P(None, "head"),
        P(None, "head"),
        P("head"),
        P("dp", SEQ, "head"),
    )
    return jax.shard_map(
        local,
        mesh=finer,
        in_specs=placed,
        out_specs=(P("dp", SEQ, "head"), P(SEQ_DP, None, "head")),
        check_vma=False,
    )
```

profile of v0, /device:TPU:1, one launch (start us, length us, event | category | flops | bytes accessed | tf_op | source)
XLA Modules:
  0.0 471.0 jit_solution(4316885514837143429)
XLA Ops:
  7.2 4.9 %fusion.38 = bf16[384,512]{1,0:T(8,128)(2,1)} fusion(bf16[3072,512]{1,0:T(8,128)(2,1)} %param.9, bf16[1,384,3072]{2,1,0:T(8,128)(2,1)} %param.6), kind=kOutput, calls=%fused_computation.37 | convolution fusion | flops 1208156160 | bytes 5898240 | tf_op jit(solution)/shard_map/dot_general | solution.py:131
  12.2 1.2 copy.68
  13.4 3.9 fusion.62
  17.3 1.4 copy.81
  18.6 1.2 fusion.71
  20.0 3.3 fusion.41
  23.5 1.3 copy.40
  24.8 22.4 %all_gather.44 = f32[8,2,256]{2,1,0:T(2,128)S(1)} all-gather(f32[1,2,256]{2,1,0:T(2,128)S(1)} %all_gather.43), channel_id=1, replica_groups=mesh['seq_0'=4,'seq_1'=8,'dp'=2,'head'=4] {'seq_1'}, dimensions={0}, use_global_device_ids=true | all-gather | bytes 18432 | tf_op jit(solution)/shard_map/all_gather | solution.py:24
  47.2 9.7 %all_gather.45 = f32[4,2,256]{2,1,0:T(2,128)S(1)} all-gather(f32[1,2,256]{2,1,0:T(2,128)S(1)} %get-tuple-element.12), channel_id=1, replica_groups=mesh['seq_0'=4,'seq_1'=8,'dp'=2,'head'=4] {'seq_0'}, dimensions={0}, use_global_device_ids=true | all-gather | bytes 10240 | tf_op jit(solution)/shard_map/all_gather | solution.py:24
  57.3 1.3 fusion.87
  58.7 19.9 %all-gather.13.cloned.1.call-done = f32[16,256,256]{2,1,0:T(8,128)} async-done(((f32[2,256,256]{2,1,0:T(8,128)}), f32[16,256,256]{2,1,0:T(8,128)}) %all-gather.13.cloned.1.call-update) | async-done | bytes 4194320 | tf_op jit(solution)/shard_map/all_gather | solution.py:24
  78.6 3.2 fusion.84
  81.9 1.0 pad_maximum_fusion
  82.9 2.2 collective-permute-start
  85.1 1.0 fusion.53
  86.0 24.6 %collective-permute-done = bf16[2,384,512]{2,1,0:T(8,128)(2,1)} collective-permute-done((bf16[2,384,512]{2,1,0:T(8,128)(2,1)}, bf16[2,384,512]{2,1,0:T(8,128)(2,1)}, u32[]{:S(2)}, u32[]{:S(2)}) %collective-permute-start) | collective-permute-done | bytes 786464 | tf_op jit(solution)/shard_map/ppermute | solution.py:37
  110.6 1.9 fusion.146
  112.7 1.2 copy.65
  114.0 0.9 copy-done.21
  114.9 2.1 fusion.92
  117.0 3.6 fusion.147
  120.6 3.5 convolution_bitcast_fusion
  124.1 22.4 %all-gather.15.cloned.1.call-done = f32[16,256,256]{2,1,0:T(8,128)} async-done(((f32[2,256,256]{2,1,0:T(8,128)}), f32[16,256,256]{2,1,0:T(8,128)}) %all-gather.15.cloned.1.call-update) | async-done | bytes 4194320 | tf_op jit(solution)/shard_map/all_gather | solution.py:24
  146.4 3.4 fusion.80
  149.9 1.2 fusion.94
  151.1 9.0 %fusion.19 = f32[768,2,256]{0,2,1:T(8,128)} fusion(bf16[384,2,256]{0,2,1:T(8,128)(2,1)S(1)} %bitcast.203, f32[2,384,768]{2,1,0:T(8,128)} %fusion.92, f32[2,384,768]{2,1,0:T(8,128)} %get-tuple-element.21, f32[2,384]{1,0:T(2,128)S(1)} %get-tuple-element.20), kind=kOutput, calls=%fused_computation.18 | convolution fusion | flops 306120192 | bytes 6687744 | tf_op jit(solution)/shard_map/hst,shd->thd/dot_general | solution.py:41
  160.1 1.2 fusion.93
  161.4 1.5 collective-permute-start.1
  162.9 10.2 %fusion.22 = f32[384,2,256]{0,2,1:T(8,128)} fusion(bf16[768,2,256]{2,0,1:T(8,128)(2,1)} %copy-done.21, f32[2,384,768]{2,1,0:T(8,128)} %fusion.92, f32[2,384,768]{2,1,0:T(8,128)} %get-tuple-element.21, f32[2,384]{1,0:T(2,128)S(1)} %get-tuple-element.20), kind=kOutput, calls=%fused_computation.20 | convolution fusion | flops 306120192 | bytes 6294528 | tf_op jit(solution)/shard_map/hst,thd->shd/dot_general | solution.py:41
  173.1 8.8 %collective-permute-done.1 = bf16[2,384,2,256]{1,3,2,0:T(8,128)(2,1)} collective-permute-done((bf16[2,384,2,256]{1,3,2,0:T(8,128)(2,1)S(1)}, bf16[2,384,2,256]{1,3,2,0:T(8,128)(2,1)}, u32[]{:S(2)}, u32[]{:S(2)}) %collective-permute-start.1) | collective-permute-done | bytes 786464 | tf_op jit(solution)/shard_map/ppermute | solution.py:37
  182.0 1.2 convert_element_type.66
  183.3 3.0 fusion.83
  186.3 1.3 multiply_reduce_fusion.1
  188.0 28.2 %all-gather.3 = f32[8,2,256]{2,1,0:T(2,128)S(1)} all-gather(f32[1,2,256]{2,1,0:T(2,128)S(1)} %bitcast.209), channel_id=4, replica_groups=mesh['seq_0'=4,'seq_1'=8,'dp'=2,'head'=4] {'seq_1'}, dimensions={0}, use_global_device_ids=true | all-gather | bytes 18432 | tf_op jit(solution)/shard_map/all_gather | solution.py:24
  216.2 9.6 %all_gather.51 = f32[4,2,256]{2,1,0:T(2,128)S(1)} all-gather(f32[1,2,256]{2,1,0:T(2,128)S(1)} %get-tuple-element.6), channel_id=1, replica_groups=mesh['seq_0'=4,'seq_1'=8,'dp'=2,'head'=4] {'seq_0'}, dimensions={0}, use_global_device_ids=true | all-gather | bytes 10240 | tf_op jit(solution)/shard_map/all_gather | solution.py:24
  225.9 2.6 all-gather.11.cloned.1.call-done
  228.5 3.2 fusion.79
  232.2 0.9 copy-done.13
  233.7 0.5 fusion.33
  234.2 1.1 copy-done.9
  235.4 10.7 %multiply_bitcast_fusion = f32[3072,1536]{0,1:T(8,128)} fusion(bf16[1,384,3072]{2,1,0:T(8,128)(2,1)S(1)} %copy-done.9, bf16[384,512]{0,1:T(8,128)(2,1)S(1)} %bitcast.198, bf16[384,512]{0,1:T(8,128)(2,1)S(1)} %bitcast.199, bf16[384,512]{0,1:T(8,128)(2,1)S(1)} %bitcast.208), kind=kOutput, calls=%fused_computation.2 | convolution fusion | flops 3632136192 | bytes 22413312 | tf_op jit(solution)/shard_map/dot_general | solution.py:183
  246.1 18.6 %copy.66 = f32[3072,1536]{1,0:T(8,128)} copy(f32[3072,1536]{0,1:T(8,128)} %multiply_bitcast_fusion) | data formatting | bytes 37748736
  264.7 0.6 copy-done.25
  265.4 3.5 fusion.34
  268.9 1.9 copy.50
  270.8 189.4 %reduce-scatter.4.cloned.1.call-done = f32[48,1536]{1,0:T(8,128)} async-done(((f32[3072,1536]{1,0:T(8,128)}), f32[48,1536]{1,0:T(8,128)}) %reduce-scatter.4.cloned.1.call-update) | async-done | bytes 294928
  460.2 2.1 copy.67
  462.3 2.1 copy.51
  (85 shorter events, 2.7 us)
Async XLA Ops:
  7.2 6.2 %copy-start = (bf16[3072,512]{1,0:T(8,128)(2,1)S(1)}, bf16[3072,512]{1,0:T(8,128)(2,1)}, u32[]{:S(2)}) copy-start(bf16[3072,512]{1,0:T(8,128)(2,1)} %param.8) | copy-start | bytes 9437188
  7.2 71.4 %all-gather.13.cloned.1.call-start = ((), (), s32[]{:S(2)}) async-start(), calls=%async_computation.3 | async-start | bytes 4718592 | tf_op jit(solution)/shard_map/all_gather | solution.py:24
  17.3 2.7 copy-start.8
  19.9 126.6 %all-gather.15.cloned.1.call-start = ((), (), s32[]{:S(2)}) async-start(), calls=%async_computation.4 | async-start | bytes 4718592 | tf_op jit(solution)/shard_map/all_gather | solution.py:24
  20.0 37.0 %copy-start.22 = (f32[2]{0:T(128)S(1)}, f32[2]{0:T(128)}, u32[]{:S(2)}) copy-start(f32[2]{0:T(128)} %param.10) | copy-start | bytes 28
  23.5 35.1 %copy-start.14 = (bf16[384,512]{0,1:T(8,128)(2,1)}, bf16[384,512]{0,1:T(8,128)(2,1)S(1)}, u32[]{:S(2)}) copy-start(bf16[384,512]{0,1:T(8,128)(2,1)S(1)} %copy.69) | copy-start | bytes 1179652
  24.8 95.8 %copy-start.5 = (f32[1,384,512]{1,2,0:T(8,128)}, f32[1,384,512]{1,2,0:T(8,128)S(1)}, u32[]{:S(2)}) copy-start(f32[1,384,512]{1,2,0:T(8,128)S(1)} %copy.40) | copy-start | bytes 2359300
  57.0 129.3 %copy-start.23 = (f32[2]{0:T(128)}, f32[2]{0:T(128)S(1)}, u32[]{:S(2)}) copy-start(f32[2]{0:T(128)S(1)} %get-tuple-element.11) | copy-start | bytes 28
  58.6 23.3 %copy-start.4 = (bf16[384,512]{1,0:T(8,128)(2,1)S(1)}, bf16[384,512]{1,0:T(8,128)(2,1)}, u32[]{:S(2)}) copy-start(bf16[384,512]{1,0:T(8,128)(2,1)} %get-tuple-element.19) | copy-start | bytes 1179652
  58.6 23.3 %copy-start.11 = (bf16[384,512]{1,0:T(8,128)(2,1)S(1)}, bf16[384,512]{1,0:T(8,128)(2,1)}, u32[]{:S(2)}) copy-start(bf16[384,512]{1,0:T(8,128)(2,1)} %fusion.38) | copy-start | bytes 1179652
  58.6 124.6 %all-gather.9.cloned.1.call-start = ((), (), s32[]{:S(2)}) async-start(), calls=%async_computation.1 | async-start | bytes 2621440 | tf_op jit(solution)/shard_map/all_gather | solution.py:24
  81.8 146.6 %all-gather.11.cloned.1.call-start = ((), (), s32[]{:S(2)}) async-start(), calls=%async_computation.2 | async-start | bytes 2621440 | tf_op jit(solution)/shard_map/all_gather | solution.py:24
  82.9 27.7 %collective-permute-start = (bf16[2,384,512]{2,1,0:T(8,128)(2,1)}, bf16[2,384,512]{2,1,0:T(8,128)(2,1)}, u32[]{:S(2)}, u32[]{:S(2)}) collective-permute-start(bf16[2,384,512]{2,1,0:T(8,128)(2,1)} %pad_maximum_fusion), channel_id=1, source_target_pairs={{0,8},{8,16},{16,24},{24,32},{32,40},{40,48},{48,56},{56,64},{64,7... | collective-permute-start | bytes 2359304 | tf_op jit(solution)/shard_map/ppermute | solution.py:37
  113.9 3.1 copy-start.10
  113.9 3.0 copy-start.15
  114.0 0.9 copy-start.21
  114.9 2.1 copy-start.18
  120.6 42.3 %copy-start.27 = (f32[2,384]{1,0:T(2,128)}, f32[2,384]{1,0:T(2,128)S(1)}, u32[]{:S(2)}) copy-start(f32[2,384]{1,0:T(2,128)S(1)} %get-tuple-element.20) | copy-start | bytes 9220
  149.9 310.3 %reduce-scatter.4.cloned.1.call-start = ((), (), s32[]{:S(2)}) async-start(), calls=%async_computation.5 | async-start | bytes 19169280
  161.4 20.5 %collective-permute-start.1 = (bf16[2,384,2,256]{1,3,2,0:T(8,128)(2,1)S(1)}, bf16[2,384,2,256]{1,3,2,0:T(8,128)(2,1)}, u32[]{:S(2)}, u32[]{:S(2)}) collective-permute-start(bf16[2,384,2,256]{1,3,2,0:T(8,128)(2,1)S(1)} %pad_maximum_fusion.2), channel_id=1, source_target_pairs={{8,0},{16,8},{24,16},{32,24},{40,32},{48,40},{56,48},{64,56},{72,6... | collective-permute-start | bytes 2359304 | tf_op jit(solution)/shard_map/ppermute | solution.py:37
  173.1 10.1 %copy-start.2 = (f32[1,2,256,256]{3,2,1,0:T(8,128)S(1)}, f32[1,2,256,256]{3,2,1,0:T(8,128)}, u32[]{:S(2)}) copy-start(f32[1,2,256,256]{3,2,1,0:T(8,128)} %get-tuple-element.14) | copy-start | bytes 1572868
  183.2 3.0 copy-start.6
  183.3 3.0 copy-start.16
  186.3 1.3 copy-start.19
  186.3 42.2 %copy-start.3 = (f32[1,2,256,256]{3,2,1,0:T(8,128)S(1)}, f32[1,2,256,256]{3,2,1,0:T(8,128)}, u32[]{:S(2)}) copy-start(f32[1,2,256,256]{3,2,1,0:T(8,128)} %get-tuple-element.8) | copy-start | bytes 1572868
  228.5 3.2 copy-start.12
  231.7 1.4 copy-start.13
  231.7 1.8 copy-start.7
  231.7 1.8 copy-start.17
  231.7 1.8 copy-start.20
  231.7 1.8 copy-start.24
  231.7 2.0 copy-start.26
  233.7 1.7 copy-start.9
  264.7 0.7 copy-start.25
  264.7 0.7 copy-start.28
  265.4 199.0 %copy-start.1 = (bf16[3072,512]{1,0:T(8,128)(2,1)S(1)}, bf16[3072,512]{1,0:T(8,128)(2,1)}, u32[]{:S(2)}) copy-start(bf16[3072,512]{1,0:T(8,128)(2,1)} %param.8) | copy-start | bytes 9437188
Sparse Core Ops, SparseCore 0:
  20.0 58.5 all-gather.12
  80.4 66.0 all-gather.14
  148.3 30.6 all-gather.8
  180.6 47.8 all-gather.10
  264.9 195.3 reduce-scatter.3
where the time goes:
time: 475 us; the launch traced here: 471 us
  waiting for transfers between devices  268 us (56%)
  blocking collectives  70 us (15%)
  matrix products  60.5 us (13%)
  local copies, waits for them, and re-layouts  38.4 us (8%)
  other arithmetic  16.2 us (3%)
  between operations  14.3 us (3%)
    unnamed x6, waiting for transfers between devices  189 us
    all_gather x4, blocking collectives, prefix_by_axis(): pieces = jax.tree.map(lambda part: lax.all_gather(part, axis), subtotal)  70 us
    all_gather x4, waiting for transfers between devices, prefix_by_axis(): pieces = jax.tree.map(lambda part: lax.all_gather(part, axis), subtotal)  44.9 us
    ppermute x2, waiting for transfers between devices, passed_along(): return lax.ppermute(x, axis, pairs)  33.4 us
    unnamed x63, local copies, waits for them, and re-layouts  28.7 us
    dot_general x5, matrix products, product(): return jnp.einsum(form, left, right, preferred_element_type=jnp.float32)  28.3 us
    add x7, other arithmetic, add_pair(): return (earlier[0] + latter[0], earlier[1] + latter[1])  12.9 us
    dot_general x3, matrix products, project(): jnp.dot(tokens, weight, preferred_element_type=jnp.float32)  12.1 us
  transfers between devices with their start and end apart: 7, of which 6 were waited for; matrix products, arithmetic and copies ran while one was open for 13% of the time, Pallas kernels for 0%

commit v1 on v0

--- a/solution.py
+++ b/solution.py
@@ -1,13 +1,200 @@
+import functools
 import math
 
 import jax
 import jax.numpy as jnp
 from jax import lax
+from jax.experimental import pallas as pl
+from jax.experimental.pallas import tpu as pltpu
 from jax.sharding import Mesh
 from jax.sharding import PartitionSpec as P
 
-SEQ = ("seq_0", "seq_1")
-SEQ_DP = ("seq_0", "seq_1", "dp")
+SEQ = ("y", "z")
+SEQ_DP = ("y", "z", "dp")
+MESH = pl.DeviceIdType.MESH
+
+
+def ring_chains(n):
+    chains, first = [], 0
+    for sub in (0, 1):
+        for way in (1, -1):
+            length = n // 2 if (way > 0) == (sub == 0) else n - 1 - n // 2
+            chains.append((sub, way, length, first))
+            first += length
+    return chains
+
+
+class RingSum:
+    def __init__(self, axis, mine, send, recv, send_sem, recv_sem):
+        self.axis, self.mine = axis, mine
+        self.n, self.position = lax.axis_size(axis), lax.axis_index(axis)
+        self.send, self.recv, self.send_sem, self.recv_sem = send, recv, send_sem, recv_sem
+        self.chains = ring_chains(self.n)
+
+    def copy(self, slot, way):
+        return pltpu.make_async_remote_copy(
+            src_ref=self.send.at[slot],
+            dst_ref=self.recv.at[slot],
+            send_sem=self.send_sem.at[slot],
+            recv_sem=self.recv_sem.at[slot],
+            device_id={self.axis: lax.rem(self.position + way + self.n, self.n)},
+            device_id_type=MESH,
+        )
+
+    def step(self, t, ahead=None):
+        for sub, way, length, first in self.chains:
+            if t >= length:
+                continue
+            if ahead is not None and (way * (length - t)) % self.n != ahead % self.n:
+                continue
+            target = lax.rem(self.position + way * (length - t) + self.n, self.n)
+            value = self.mine(target, sub)
+            if t:
+                self.copy(first + t - 1, way).wait_recv()
+                value = value + self.recv[first + t - 1].astype(jnp.float32)
+            self.send[first + t] = value.astype(jnp.bfloat16)
+            self.copy(first + t, way).start()
+
+    def total(self, sub):
+        value = self.mine(self.position, sub)
+        for chain_sub, way, length, first in self.chains:
+            if chain_sub == sub and length:
+                self.copy(first + length - 1, way).wait_recv()
+                value = value + self.recv[first + length - 1].astype(jnp.float32)
+        return value
+
+    def drain(self):
+        for _, way, length, first in self.chains:
+            for t in range(length):
+                self.copy(first + t, way).wait_send()
+
+
+def weight_kernel(
+    scale, x_ref, g_ref, out_ref, x_all, g_all, dw, a_sum, b_sum, fin, swap,
+    a1_send, a1_recv, b1_send, b1_recv, a2_send, a2_recv, b2_send, b2_recv,
+    local_sem, pair_sem, z1_sem, y1_sem, y2_sem, z2_sem,
+):
+    ny, nz = lax.axis_size("y"), lax.axis_size("z")
+    y, dp = lax.axis_index("y"), lax.axis_index("dp")
+    other = {"dp": 1 - dp}
+    tokens = x_ref.shape[0]
+    half = g_ref.shape[2] // 2
+    wide = dw.shape[1]
+    block = wide // nz
+    rows = block // 2
+
+    barrier = pltpu.get_barrier_semaphore()
+    pl.semaphore_signal(barrier, inc=1, device_id=other, device_id_type=MESH)
+    for axis, n in (("y", ny), ("z", nz)):
+        for way in (1, -1):
+            seat = lax.rem(lax.axis_index(axis) + way + n, n)
+            pl.semaphore_signal(barrier, inc=1, device_id={axis: seat}, device_id_type=MESH)
+    x_in = pltpu.make_async_copy(x_ref, x_all.at[pl.ds(0, tokens)], local_sem.at[0])
+    g_in = pltpu.make_async_copy(g_ref.at[dp], g_all.at[pl.ds(0, tokens)], local_sem.at[1])
+    x_in.start()
+    g_in.start()
+    pl.semaphore_wait(barrier, 5)
+
+    def pair_copy(src, dst, slot):
+        return pltpu.make_async_remote_copy(
+            src_ref=src, dst_ref=dst, send_sem=pair_sem.at[0, slot], recv_sem=pair_sem.at[1, slot],
+            device_id=other, device_id_type=MESH,
+        )
+
+    g_out = pair_copy(g_ref.at[1 - dp], g_all.at[pl.ds(tokens, tokens)], 0)
+    x_out = pair_copy(x_ref, x_all.at[pl.ds(tokens, tokens)], 1)
+    g_out.start()
+    x_out.start()
+    x_in.wait()
+    g_in.wait()
+    g_out.wait_recv()
+    x_out.wait_recv()
+
+    tile = min(wide, 256)
+
+    def products(target):
+        def body(i, carry):
+            start = pl.multiple_of(target * wide + i * tile, 128)
+            dw[target, pl.ds(pl.multiple_of(i * tile, 8), tile), :] = lax.dot_general(
+                x_all[:, pl.ds(start, tile)], g_all[...], (((0,), (0,)), ((), ())),
+                preferred_element_type=jnp.float32,
+            )
+            return carry
+        lax.fori_loop(0, wide // tile, body, 0)
+
+    def a1_mine(target, sub):
+        return dw[:, pl.ds(pl.multiple_of(target * block + sub * rows, 8), rows), :half]
+
+    def b1_mine(target, sub):
+        return dw[target, sub * (wide // 2):(sub + 1) * (wide // 2), half:]
+
+    def b2_mine(target, sub):
+        return b_sum[pl.ds(pl.multiple_of(target * block + sub * rows, 8), rows), :]
+
+    a1 = RingSum("z", a1_mine, a1_send, a1_recv, z1_sem.at[0], z1_sem.at[1])
+    b1 = RingSum("y", b1_mine, b1_send, b1_recv, y1_sem.at[0], y1_sem.at[1])
+    a2 = RingSum("y", lambda k, sub: a_sum[sub, k], a2_send, a2_recv, y2_sem.at[0], y2_sem.at[1])
+    b2 = RingSum("z", b2_mine, b2_send, b2_recv, z2_sem.at[0], z2_sem.at[1])
+
+    for step in range(ny):
+        ahead = ny // 2 - step
+        products(lax.rem(y + ahead + ny, ny))
+        b1.step(0, ahead)
+    a1.step(0)
+    a1.step(1)
+    b1.step(1)
+    for t in range(2, nz // 2):
+        a1.step(t)
+    for sub in (0, 1):
+        b_sum[sub * (wide // 2):(sub + 1) * (wide // 2), :] = b1.total(sub)
+    b2.step(0)
+    for sub in (0, 1):
+        a_sum[sub] = a1.total(sub)
+    for t in range(max(ny, nz) // 2):
+        a2.step(t)
+        b2.step(t + 1)
+    for sub in (0, 1):
+        fin[sub, :, :half] = a2.total(sub) * scale
+        fin[sub, :, half:] = b2.total(sub) * scale
+    swap_out = pair_copy(fin.at[1 - dp], swap, 2)
+    swap_out.start()
+    out_ref[dp] = fin[dp]
+    for ring in (a1, b1, a2, b2):
+        ring.drain()
+    g_out.wait_send()
+    x_out.wait_send()
+    swap_out.wait()
+    out_ref[1 - dp] = swap[...]
+
+
+def weight_sum(x, g, scale):
+    tokens, depth = x.shape
+    cols = g.shape[2]
+    ny, nz = lax.axis_size("y"), lax.axis_size("z")
+    wide = depth // ny
+    rows = wide // nz // 2
+    half = cols // 2
+    zs, ys = 2 * (nz - 1), 2 * (ny - 1)
+    wire = lambda *shape: pltpu.VMEM(shape, jnp.bfloat16)
+    real = lambda *shape: pltpu.VMEM(shape, jnp.float32)
+    dma = lambda *shape: pltpu.SemaphoreType.DMA(shape)
+    a1, b1, last = (zs, ny, rows, half), (ys, wide // 2, half), (rows, half)
+    return pl.pallas_call(
+        functools.partial(weight_kernel, scale),
+        out_shape=jax.ShapeDtypeStruct((2, rows, cols), jnp.float32),
+        in_specs=[pl.BlockSpec(memory_space=pl.ANY)] * 2,
+        out_specs=pl.BlockSpec(memory_space=pltpu.VMEM),
+        scratch_shapes=[
+            wire(2 * tokens, depth), wire(2 * tokens, cols), real(ny, wide, cols),
+            real(2, ny, rows, half), real(wide, half), real(2, rows, cols), real(rows, cols),
+            wire(*a1), wire(*a1), wire(*b1), wire(*b1),
+            wire(ys, *last), wire(ys, *last), wire(zs, *last), wire(zs, *last),
+            dma(2), dma(2, 3), dma(2, zs), dma(2, ys), dma(2, ys), dma(2, zs),
+        ],
+        compiler_params=pltpu.CompilerParams(
+            collective_id=1, has_side_effects=True, vmem_limit_bytes=60 * 1024 * 1024
+        ),
+    )(x, g)
 
 
 def filled_with(x, identity):
@@ -167,33 +354,19 @@
     grad_key = (grad_keys[seg_len:] + incoming[0] + write_key).astype(jnp.bfloat16)
     grad_value = (grad_values[seg_len:] + incoming[1] + write_value).astype(jnp.bfloat16)
     grad_all = jnp.concatenate(
-        [
-            grad_query.astype(jnp.bfloat16).reshape(seg_len, columns),
-            grad_key.reshape(seg_len, columns),
-            grad_value.reshape(seg_len, columns),
-        ],
-        1,
-    )
-    seq_count = lax.axis_size(SEQ)
-    dp_count = lax.axis_size("dp")
-    grad_scale = 1.0 / math.sqrt(seq_count * dp_count * seg_len)
-    part_rows = model_dim // (seq_count * dp_count)
-    contract = (((0,), (0,)), ((), ()))
-    summed = lax.psum_scatter(
-        lax.dot_general(tokens, grad_all, contract, preferred_element_type=jnp.float32)
-        * grad_scale,
-        SEQ_DP,
-        scatter_dimension=0,
-        tiled=True,
-    )
-    grad_weights = summed.reshape(part_rows, 3, columns)
+        [grad_query.astype(jnp.bfloat16), grad_key, grad_value], 2
+    ).transpose(1, 0, 2)
+    scale = 1.0 / math.sqrt(lax.axis_size(SEQ) * lax.axis_size("dp") * seg_len)
+    summed = weight_sum(tokens, grad_all, scale)
+    rows = summed.shape[1]
+    grad_weights = summed.reshape(2, rows, 3, head_dim).transpose(1, 2, 0, 3).reshape(rows, 3, columns)
     return (blended.reshape(1, seg_len, columns), grad_weights)
 
 
 def solution(mesh):
     finer = Mesh(
         mesh.devices.reshape(4, 8, mesh.shape["dp"], mesh.shape["head"]),
-        ("seq_0", "seq_1", "dp", "head"),
+        ("y", "z", "dp", "head"),
     )
     placed = (
         P("dp", SEQ, None),

time: 475 us -> 311 us (0.65)
  waiting for transfers between devices: 268 us -> 53.3 us
  Pallas kernels: 0 us -> 59.8 us
  local copies, waits for them, and re-layouts: 38.4 us -> 29.8 us
  matrix products: 60.5 us -> 54 us
  other arithmetic: 16.2 us -> 21.6 us
    unnamed x6 -> x4, waiting for transfers between devices: 189 us -> 0.07 us
    pallas_call x0 -> x1, Pallas kernels: none -> 59.8 us  [weight_sum(): pl.pallas_call(functools.partial(weight_kernel, scale), out_shape=jax.Sha...]
    all_gather x4, waiting for transfers between devices: 44.9 us -> 16.8 us  [prefix_by_axis(): pieces = jax.tree.map(lambda part: lax.all_gather(part, axis), subtotal)]
    unnamed x63 -> x43, local copies, waits for them, and re-layouts: 28.7 us -> 4.63 us
    dot_general x1 -> x0, matrix products: 10.7 us -> none  [local(): lax.dot_general(tokens, grad_all, contract, preferred_element_type=jnp.fl...]
  transfers between devices with their start and end apart: 7 -> 6, of which waited for: 6 -> 5; matrix products, arithmetic and copies ran while one was open for 13% -> 25% of each run, Pallas kernels for 0% -> 0%
where the time goes in v1:
time: 311 us; the launch traced here: 310 us
  blocking collectives  73.5 us (24%)
  Pallas kernels  59.8 us (19%)
  matrix products  54 us (17%)
  waiting for transfers between devices  53.3 us (17%)
  local copies, waits for them, and re-layouts  29.8 us (10%)
  other arithmetic  21.6 us (7%)
  between operations  14.1 us (5%)
  starting transfers between devices  3.8 us (1%)
    all_gather x4, blocking collectives, prefix_by_axis(): pieces = jax.tree.map(lambda part: lax.all_gather(part, axis), subtotal)  73.5 us
    pallas_call x1, Pallas kernels, weight_sum(): pl.pallas_call(functools.partial(weight_kernel, scale), out_shape=jax.Sha...  59.8 us
    ppermute x2, waiting for transfers between devices, passed_along(): return lax.ppermute(x, axis, pairs)  36.4 us
    dot_general x5, matrix products, product(): return jnp.einsum(form, left, right, preferred_element_type=jnp.float32)  27.8 us
    all_gather x4, waiting for transfers between devices, prefix_by_axis(): pieces = jax.tree.map(lambda part: lax.all_gather(part, axis), subtotal)  16.8 us
    dot_general x3, matrix products, project(): jnp.dot(tokens, weight, preferred_element_type=jnp.float32)  13.5 us
    add x7, other arithmetic, add_pair(): return (earlier[0] + latter[0], earlier[1] + latter[1])  13.3 us
  transfers between devices with their start and end apart: 6, of which 5 were waited for; matrix products, arithmetic and copies ran while one was open for 25% of the time, Pallas kernels for 0%

profile of v1, /device:TPU:1, one launch (start us, length us, event | category | flops | bytes accessed | tf_op | source)
XLA Modules:
  0.0 310.0 jit_solution(1243740417877781703)
XLA Ops:
  7.2 4.9 %convolution_convert_fusion.1 = bf16[384,512]{1,0:T(8,128)(2,1)} fusion(bf16[3072,512]{1,0:T(8,128)(2,1)} %param.9, bf16[1,384,3072]{2,1,0:T(8,128)(2,1)} %param.6), kind=kOutput, calls=%fused_computation.29 | convolution fusion | flops 1208156160 | bytes 5898240 | tf_op jit(solution)/shard_map/dot_general | solution.py:318
  12.1 1.2 copy.141
  13.3 3.9 %fusion.41 = (f32[512]{0:T(512)S(1)}, bf16[384,512]{1,0:T(8,128)(2,1)}) fusion(bf16[3072,512]{1,0:T(8,128)(2,1)S(1)} %copy-done, bf16[1,384,3072]{2,1,0:T(8,128)(2,1)} %param.6), kind=kOutput, calls=%fused_computation.56 | convolution fusion | flops 1209335296 | bytes 5900288 | tf_op jit(solution)/shard_map/dot_general | solution.py:318
  17.3 1.9 copy.90
  19.2 1.9 copy.91
  21.1 2.2 fusion.50
  23.4 4.7 %convolution_convert_fusion = bf16[384,512]{1,0:T(8,128)(2,1)} fusion(bf16[3072,512]{1,0:T(8,128)(2,1)} %param.7, bf16[1,384,3072]{2,1,0:T(8,128)(2,1)} %param.6), kind=kOutput, calls=%fused_computation.28 | convolution fusion | flops 1208156160 | bytes 5898240 | tf_op jit(solution)/shard_map/dot_general | solution.py:318
  28.2 1.9 copy.94
  30.1 1.9 copy.95
  32.1 2.1 copy.103
  34.1 24.0 %all_gather.44 = f32[8,2,256]{2,1,0:T(2,128)S(1)} all-gather(f32[1,2,256]{2,1,0:T(2,128)S(1)} %all_gather.43), channel_id=1, replica_groups=mesh['y'=4,'z'=8,'dp'=2,'head'=4] {'z'}, dimensions={0}, use_global_device_ids=true | all-gather | bytes 18432 | tf_op jit(solution)/shard_map/all_gather | solution.py:211
  58.1 9.7 %all_gather.45 = f32[4,2,256]{2,1,0:T(2,128)S(1)} all-gather(f32[1,2,256]{2,1,0:T(2,128)S(1)} %get-tuple-element.16), channel_id=1, replica_groups=mesh['y'=4,'z'=8,'dp'=2,'head'=4] {'y'}, dimensions={0}, use_global_device_ids=true | all-gather | bytes 10240 | tf_op jit(solution)/shard_map/all_gather | solution.py:211
  68.4 1.3 fusion.68
  69.7 2.5 fusion.66
  72.4 9.8 %all-gather.13.cloned.1.call-done = f32[16,256,256]{2,1,0:T(8,128)} async-done(((f32[2,256,256]{2,1,0:T(8,128)}), f32[16,256,256]{2,1,0:T(8,128)}) %all-gather.13.cloned.1.call-update) | async-done | bytes 4194320 | tf_op jit(solution)/shard_map/all_gather | solution.py:211
  82.2 3.4 %fusion.63 = (f32[1,2,256,256]{3,2,1,0:T(8,128)}, f32[2,256,256]{2,1,0:T(8,128)}) fusion(f32[16,256,256]{2,1,0:T(8,128)} %all-gather.13.cloned.1.call-done), kind=kLoop, calls=%fused_computation.99 | loop fusion | flops 917504 | bytes 5242880 | tf_op jit(solution)/shard_map/add | solution.py:240
  85.7 2.2 pad_maximum_fusion
  87.9 2.2 collective-permute-start
  91.0 26.2 %collective-permute-done = bf16[2,384,512]{2,1,0:T(8,128)(2,1)} collective-permute-done((bf16[2,384,512]{2,1,0:T(8,128)(2,1)}, bf16[2,384,512]{2,1,0:T(8,128)(2,1)}, u32[]{:S(2)}, u32[]{:S(2)}) %collective-permute-start) | collective-permute-done | bytes 786464 | tf_op jit(solution)/shard_map/ppermute | solution.py:224
  117.2 2.1 fusion.130
  119.2 1.9 copy.99
  121.2 1.9 copy.100
  123.1 1.9 copy.140
  125.0 4.5 %fusion.131 = (f32[2,384]{1,0:T(2,128)}, f32[2,384,768]{2,1,0:T(8,128)}) fusion(pred[384,768]{1,0:T(8,128)(4,1)} %fusion.32, bf16[384,2,256]{0,2,1:T(8,128)(2,1)} %bitcast.179, bf16[384,2,256]{2,0,1:T(8,128)(2,1)} %copy.91, bf16[384,2,256]{2,0,1:T(8,128)(2,1)} %copy.100), kind=kOutput, calls=%fused_computation.198 | convolution fusion | flops 305922816 | bytes 3836928 | tf_op jit(solution)/shard_map/sub | solution.py:272
  129.5 3.3 %fusion.72 = f32[2,384,768]{2,1,0:T(8,128)} fusion(bf16[384,2,256]{0,2,1:T(8,128)(2,1)S(1)} %bitcast.167, bf16[384,2,256]{0,2,1:T(8,128)(2,1)} %bitcast.176, f32[384,2,256]{0,2,1:T(8,128)} %bitcast.171, f32[2]{0:T(128)S(1)} %copy-done.12), kind=kOutput, calls=%fused_computation.112 | convolution fusion | flops 303955968 | bytes 3932168 | tf_op jit(solution)/shard_map/shd,thd->hst/dot_general | solution.py:228
  132.8 10.2 %fusion.12 = f32[768,2,256]{2,0,1:T(8,128)} fusion(bf16[384,2,256]{0,2,1:T(8,128)(2,1)} %bitcast.180, f32[2,384,768]{2,1,0:T(8,128)} %fusion.72, f32[2,384,768]{2,1,0:T(8,128)} %get-tuple-element.25, f32[2,384]{1,0:T(2,128)} %get-tuple-element.24), kind=kOutput, calls=%fused_computation.10 | convolution fusion | flops 306120192 | bytes 6687744 | tf_op jit(solution)/shard_map/hst,shd->thd/dot_general | solution.py:228
  143.1 3.8 %convolution_bitcast_fusion = f32[768,2,256]{2,0,1:T(8,128)} fusion(f32[384,2,256]{0,2,1:T(8,128)} %bitcast.172, f32[2]{0:T(128)S(1)} %copy-done.12, f32[2,384,768]{2,1,0:T(8,128)} %get-tuple-element.25, f32[2,384]{1,0:T(2,128)} %get-tuple-element.24), kind=kOutput, calls=%fused_computation.11 | convolution fusion | flops 303562752 | bytes 4721672 | tf_op jit(solution)/shard_map/hst,shd->thd/dot_general | solution.py:228
  146.9 4.5 %all-gather.15.cloned.1.call-done = f32[16,256,256]{2,1,0:T(8,128)} async-done(((f32[2,256,256]{2,1,0:T(8,128)}), f32[16,256,256]{2,1,0:T(8,128)}) %all-gather.15.cloned.1.call-update) | async-done | bytes 4194320 | tf_op jit(solution)/shard_map/all_gather | solution.py:211
  151.4 3.4 %fusion.59 = (f32[1,2,256,256]{3,2,1,0:T(8,128)}, f32[2,256,256]{2,1,0:T(8,128)}) fusion(f32[16,256,256]{2,1,0:T(8,128)} %all-gather.15.cloned.1.call-done), kind=kLoop, calls=%fused_computation.85 | loop fusion | flops 917504 | bytes 5242880 | tf_op jit(solution)/shard_map/add | solution.py:240
  154.9 1.2 fusion.74
  156.1 1.2 fusion.73
  157.2 1.0 pad_maximum_fusion.3
  158.2 1.5 collective-permute-start.1
  159.7 9.0 %fusion.15 = f32[384,2,256]{2,0,1:T(8,128)} fusion(f32[2,384,768]{2,1,0:T(8,128)} %fusion.72, bf16[384,2,256]{2,0,1:T(8,128)(2,1)} %copy.91, bf16[384,2,256]{2,0,1:T(8,128)(2,1)} %copy.100, f32[2,384,768]{2,1,0:T(8,128)} %get-tuple-element.25, f32[2,384]{1,0:T(2,128)} %get-tuple-element.24), kind=kOutput, calls=%fused_computation.12 | convolution fusion | flops 307693056 | bytes 6294528 | tf_op jit(solution)/shard_map/hst,thd->shd/dot_general | solution.py:228
  168.7 10.3 %collective-permute-done.1 = bf16[2,384,2,256]{3,1,2,0:T(8,128)(2,1)} collective-permute-done((bf16[2,384,2,256]{3,1,2,0:T(8,128)(2,1)}, bf16[2,384,2,256]{3,1,2,0:T(8,128)(2,1)}, u32[]{:S(2)}, u32[]{:S(2)}) %collective-permute-start.1) | collective-permute-done | bytes 786464 | tf_op jit(solution)/shard_map/ppermute | solution.py:224
  179.0 2.4 convert_element_type.66
  181.4 2.4 all-gather.9.cloned.1.call-done
  183.8 3.2 %fusion.62 = bf16[2,256,256]{2,1,0:T(8,128)(2,1)S(1)} fusion(f32[4,2,256,256]{3,2,1,0:T(8,128)} %all-gather.9.cloned.1.call-done, f32[1,2,256,256]{3,2,1,0:T(8,128)} %get-tuple-element.18, f32[2,256,256]{2,1,0:T(8,128)} %get-tuple-element.19, f32[16,256,256]{2,1,0:T(8,128)} %all-gather.13.cloned.1.call-done, pred[]{:T(512)S(6)} %gt.57, pred[]{:T(512)S(6)} %gt.58, ...), kind=kLoop, calls=%fused_computation.95 | loop fusion | flops 2883584 | bytes 6553612 | tf_op jit(solution)/shard_map/add | solution.py:240
  188.9 1.4 fusion.27
  190.4 1.9 copy.119
  192.3 31.1 %all-gather.3 = f32[8,2,256]{2,1,0:T(2,128)S(1)} all-gather(f32[1,2,256]{2,1,0:T(2,128)S(1)} %bitcast.187), channel_id=4, replica_groups=mesh['y'=4,'z'=8,'dp'=2,'head'=4] {'z'}, dimensions={0}, use_global_device_ids=true | all-gather | bytes 18432 | tf_op jit(solution)/shard_map/all_gather | solution.py:211
  223.4 8.7 %all_gather.51 = f32[4,2,256]{2,1,0:T(2,128)S(1)} all-gather(f32[1,2,256]{2,1,0:T(2,128)S(1)} %get-tuple-element.10), channel_id=1, replica_groups=mesh['y'=4,'z'=8,'dp'=2,'head'=4] {'y'}, dimensions={0}, use_global_device_ids=true | all-gather | bytes 10240 | tf_op jit(solution)/shard_map/all_gather | solution.py:211
  232.2 3.2 %fusion.58 = bf16[2,256,256]{2,1,0:T(8,128)(2,1)S(1)} fusion(f32[4,2,256,256]{3,2,1,0:T(8,128)} %all-gather.11.cloned.1.call-done, f32[1,2,256,256]{3,2,1,0:T(8,128)} %get-tuple-element.12, f32[2,256,256]{2,1,0:T(8,128)} %get-tuple-element.13, f32[16,256,256]{2,1,0:T(8,128)} %all-gather.15.cloned.1.call-done, pred[]{:T(512)S(6)} %lt.41, pred[]{:T(512)S(6)} %lt.42, ...), kind=kLoop, calls=%fused_computation.81 | loop fusion | flops 2883584 | bytes 6553612 | tf_op jit(solution)/shard_map/add | solution.py:240
  236.3 1.0 copy-done.6
  238.5 1.1 maximum_bitcast_fusion.g_ref
  239.6 59.8 %shard_map.77 = f32[2,48,768]{2,1,0:T(8,128)} custom-call(bf16[384,3072]{1,0:T(8,128)(2,1)} %bitcast.175, bf16[2,384,768]{2,1,0:T(8,128)(2,1)} %maximum_bitcast_fusion.g_ref), custom_call_target="tpu_custom_call" | custom-call | tf_op jit(solution)/shard_map/pallas_call | solution.py:182
  299.5 1.1 reshape.143
  301.5 1.9 reshape.144
  (68 shorter events, 6.6 us)
Async XLA Ops:
  7.2 6.2 %copy-start = (bf16[3072,512]{1,0:T(8,128)(2,1)S(1)}, bf16[3072,512]{1,0:T(8,128)(2,1)}, u32[]{:S(2)}) copy-start(bf16[3072,512]{1,0:T(8,128)(2,1)} %param.8) | copy-start | bytes 9437188
  7.2 75.0 %all-gather.13.cloned.1.call-start = ((), (), s32[]{:S(2)}) async-start(), calls=%async_computation.2 | async-start | bytes 4718592 | tf_op jit(solution)/shard_map/all_gather | solution.py:211
  23.4 128.0 %all-gather.15.cloned.1.call-start = ((), (), s32[]{:S(2)}) async-start(), calls=%async_computation.3 | async-start | bytes 4718592 | tf_op jit(solution)/shard_map/all_gather | solution.py:211
  28.2 39.7 %copy-start.14 = (f32[2]{0:T(128)S(1)}, f32[2]{0:T(128)}, u32[]{:S(2)}) copy-start(f32[2]{0:T(128)} %param.10) | copy-start | bytes 28
  68.4 1.3 copy-start.15
  72.3 111.5 %all-gather.9.cloned.1.call-start = ((), (), s32[]{:S(2)}) async-start(), calls=%async_computation | async-start | bytes 2621440 | tf_op jit(solution)/shard_map/all_gather | solution.py:211
  85.6 146.6 %all-gather.11.cloned.1.call-start = ((), (), s32[]{:S(2)}) async-start(), calls=%async_computation.1 | async-start | bytes 2621440 | tf_op jit(solution)/shard_map/all_gather | solution.py:211
  87.9 29.3 %collective-permute-start = (bf16[2,384,512]{2,1,0:T(8,128)(2,1)}, bf16[2,384,512]{2,1,0:T(8,128)(2,1)}, u32[]{:S(2)}, u32[]{:S(2)}) collective-permute-start(bf16[2,384,512]{2,1,0:T(8,128)(2,1)} %pad_maximum_fusion), channel_id=1, source_target_pairs={{0,8},{8,16},{16,24},{24,32},{32,40},{40,48},{48,56},{56,64},{64,7... | collective-permute-start | bytes 2359304 | tf_op jit(solution)/shard_map/ppermute | solution.py:224
  125.0 4.5 %copy-start.12 = (f32[2]{0:T(128)S(1)}, f32[2]{0:T(128)}, u32[]{:S(2)}) copy-start(f32[2]{0:T(128)} %get-tuple-element.14) | copy-start | bytes 28
  158.2 20.7 %collective-permute-start.1 = (bf16[2,384,2,256]{3,1,2,0:T(8,128)(2,1)}, bf16[2,384,2,256]{3,1,2,0:T(8,128)(2,1)}, u32[]{:S(2)}, u32[]{:S(2)}) collective-permute-start(bf16[2,384,2,256]{3,1,2,0:T(8,128)(2,1)} %pad_maximum_fusion.3), channel_id=1, source_target_pairs={{8,0},{16,8},{24,16},{32,24},{40,32},{48,40},{56,48},{64,56},{72,6... | collective-permute-start | bytes 2359304 | tf_op jit(solution)/shard_map/ppermute | solution.py:224
  183.8 3.2 %copy-start.3 = (f32[1,384,512]{1,2,0:T(8,128)S(1)}, f32[1,384,512]{1,2,0:T(8,128)}, u32[]{:S(2)}) copy-start(f32[1,384,512]{1,2,0:T(8,128)} %copy.103) | copy-start | bytes 2359300
  183.8 3.2 %copy-start.8 = (bf16[384,2,256]{2,0,1:T(8,128)(2,1)S(1)}, bf16[384,2,256]{2,0,1:T(8,128)(2,1)}, u32[]{:S(2)}) copy-start(bf16[384,2,256]{2,0,1:T(8,128)(2,1)} %copy.95) | copy-start | bytes 1179652
  183.8 3.2 %copy-start.16 = (f32[2]{0:T(128)S(1)}, f32[2]{0:T(128)}, u32[]{:S(2)}) copy-start(f32[2]{0:T(128)} %copy-done.15) | copy-start | bytes 28
  187.0 0.7 copy-start.10
  187.0 1.1 copy-start.5
  187.1 1.1 copy-start.13
  187.1 1.9 copy-start.18
  187.1 1.9 copy-start.20
  232.2 3.3 %copy-start.1 = (f32[2,384,2,256]{3,1,2,0:T(8,128)S(1)}, f32[2,384,2,256]{3,1,2,0:T(8,128)}, u32[]{:S(2)}) copy-start(f32[2,384,2,256]{3,1,2,0:T(8,128)} %convert_element_type.66) | copy-start | bytes 4718596
  232.2 3.3 %copy-start.2 = (bf16[384,2,256]{2,0,1:T(8,128)(2,1)S(1)}, bf16[384,2,256]{2,0,1:T(8,128)(2,1)}, u32[]{:S(2)}) copy-start(bf16[384,2,256]{2,0,1:T(8,128)(2,1)} %copy.91) | copy-start | bytes 1179652
  232.2 3.7 %copy-start.7 = (f32[768,2,256]{2,0,1:T(8,128)S(1)}, f32[768,2,256]{2,0,1:T(8,128)}, u32[]{:S(2)}) copy-start(f32[768,2,256]{2,0,1:T(8,128)} %convolution_bitcast_fusion) | copy-start | bytes 4718596
  235.9 1.4 copy-start.6
  235.9 1.9 copy-start.4
  235.9 1.9 copy-start.9
  235.9 1.9 copy-start.11
  235.9 1.9 copy-start.17
  235.9 2.0 copy-start.19
Sparse Core Ops, SparseCore 0:
  23.5 58.6 all-gather.12
  84.0 67.3 all-gather.14
  153.2 30.5 all-gather.8
  185.5 44.6 all-gather.10

commit v2 on v1

v2 whole, which is shorter than its diff:
```python
import functools
import math

import jax
import jax.numpy as jnp
from jax import lax
from jax.experimental import pallas as pl
from jax.experimental.pallas import tpu as pltpu
from jax.sharding import Mesh
from jax.sharding import PartitionSpec as P

SEQ = ("y", "z")
SEQ_DP = ("y", "z", "dp")
MESH = pl.DeviceIdType.MESH
MASKED = -1e30


def feature(u):
    return jnp.where(u > 0, u + 1.0, jnp.exp(jnp.minimum(u, 0.0)))


def feature_slope(u):
    return jnp.where(u > 0, 1.0, jnp.exp(jnp.minimum(u, 0.0)))


def contract(a, b, over_a, over_b):
    return lax.dot_general(
        a, b, (((over_a,), (over_b,)), ((), ())), preferred_element_type=jnp.float32
    )


def dot_nn(a, b):
    return contract(a, b, 1, 0)


def dot_nt(a, b):
    return contract(a, b, 1, 1)


def dot_tn(a, b):
    return contract(a, b, 0, 0)


def ring_chains(n):
    chains, first = [], 0
    for sub in (0, 1):
        for way in (1, -1):
            length = n // 2 if (way > 0) == (sub == 0) else n - 1 - n // 2
            chains.append((sub, way, length, first))
            first += length
    return chains


class RingSum:
    def __init__(self, axis, mine, send, recv, send_sem, recv_sem):
        self.axis, self.mine = axis, mine
        self.n, self.position = lax.axis_size(axis), lax.axis_index(axis)
        self.send, self.recv, self.send_sem, self.recv_sem = send, recv, send_sem, recv_sem
        self.chains = ring_chains(self.n)

    def copy(self, slot, way):
        return pltpu.make_async_remote_copy(
            src_ref=self.send.at[slot],
            dst_ref=self.recv.at[slot],
            send_sem=self.send_sem.at[slot],
            recv_sem=self.recv_sem.at[slot],
            device_id={self.axis: lax.rem(self.position + way + self.n, self.n)},
            device_id_type=MESH,
        )

    def step(self, t, ahead=None):
        for sub, way, length, first in self.chains:
            if t >= length:
                continue
            if ahead is not None and (way * (length - t)) % self.n != ahead % self.n:
                continue
            target = lax.rem(self.position + way * (length - t) + self.n, self.n)
            value = self.mine(target, sub)
            if t:
                self.copy(first + t - 1, way).wait_recv()
                value = value + self.recv[first + t - 1].astype(jnp.float32)
            self.send[first + t] = value.astype(jnp.bfloat16)
            self.copy(first + t, way).start()

    def total(self, sub):
        value = self.mine(self.position, sub)
        for chain_sub, way, length, first in self.chains:
            if chain_sub == sub and length:
                self.copy(first + length - 1, way).wait_recv()
                value = value + self.recv[first + length - 1].astype(jnp.float32)
        return value

    def drain(self):
        for _, way, length, first in self.chains:
            for t in range(length):
                self.copy(first + t, way).wait_send()


class Spread:
    def __init__(self, axis, got, sem):
        self.axis, self.got, self.sem = axis, got, sem
        self.n, self.position = lax.axis_size(axis), lax.axis_index(axis)

    def copy(self, src, j):
        return pltpu.make_async_remote_copy(
            src_ref=src,
            dst_ref=self.got.at[j],
            send_sem=self.sem.at[0, j],
            recv_sem=self.sem.at[1, j],
            device_id={self.axis: lax.rem(self.position + j, self.n)},
            device_id_type=MESH,
        )

    def start(self, src):
        self.src = src
        for j in range(1, self.n):
            self.copy(src, j).start()

    def sums(self, own, reverse):
        passed, total = jnp.zeros_like(own), own
        for j in range(1, self.n):
            self.copy(self.src, j).wait_recv()
            value = self.got[j]
            earlier = self.position < j if reverse else self.position >= j
            passed = passed + value * jnp.where(earlier, 1.0, 0.0)
            total = total + value
        return passed, total

    def drain(self):
        for j in range(1, self.n):
            self.copy(self.src, j).wait_send()


class VectorScan:
    def __init__(self, reverse, own, z_got, y_own, y_got, z_sem, y_sem):
        self.reverse, self.own, self.y_own = reverse, own, y_own
        self.z, self.y = Spread("z", z_got, z_sem), Spread("y", y_got, y_sem)

    def start(self):
        self.z.start(self.own)

    def across_rows(self):
        self.inside, total = self.z.sums(self.own[...], self.reverse)
        self.y_own[...] = total
        self.y.start(self.y_own)

    def result(self):
        passed, _ = self.y.sums(self.y_own[...], self.reverse)
        return passed + self.inside

    def drain(self):
        self.z.drain()
        self.y.drain()


class MemoryScan:
    def __init__(self, reverse, parts, got, inside, y_own, y_got, back, result, z_sem, y_sem, back_sem):
        self.reverse, self.parts, self.got, self.inside, self.y_own = reverse, parts, got, inside, y_own
        self.back, self.full, self.z_sem, self.back_sem = back, result, z_sem, back_sem
        self.n, self.position = lax.axis_size("z"), lax.axis_index("z")
        self.y = Spread("y", y_got, y_sem)

    def out_copy(self, j):
        target = lax.rem(self.position + j, self.n)
        return pltpu.make_async_remote_copy(
            src_ref=self.parts.at[target],
            dst_ref=self.got.at[j],
            send_sem=self.z_sem.at[0, j],
            recv_sem=self.z_sem.at[1, j],
            device_id={"z": target},
            device_id_type=MESH,
        )

    def back_copy(self, j):
        target = lax.rem(self.position + j, self.n)
        return pltpu.make_async_remote_copy(
            src_ref=self.back.at[target],
            dst_ref=self.full.at[self.position],
            send_sem=self.back_sem.at[0, j],
            recv_sem=self.back_sem.at[1, j],
            device_id={"z": target},
            device_id_type=MESH,
        )

    def start(self):
        for j in range(1, self.n):
            self.out_copy(j).start()

    def across_rows(self):
        for j in range(1, self.n):
            self.out_copy(j).wait_recv()
        self.got[0] = self.parts[self.position]
        run = jnp.zeros(self.y_own.shape, jnp.float32)
        for k in reversed(range(self.n)) if self.reverse else range(self.n):
            self.inside[k] = run
            run = run + self.got[lax.rem(self.position - k + self.n, self.n)].astype(jnp.float32)
        self.y_own[...] = run
        self.y.start(self.y_own)

    def give_back(self):
        passed, _ = self.y.sums(self.y_own[...], self.reverse)
        for k in range(self.n):
            self.back[k] = (self.inside[k] + passed).astype(jnp.bfloat16)
        for j in range(1, self.n):
            self.back_copy(j).start()
        self.full[self.position] = self.back[self.position]

    def finish(self):
        for j in range(1, self.n):
            self.back_copy(j).wait_recv()

    def head(self, h, heads):
        parts = self.n // heads
        block = self.full[pl.ds(h * parts, parts)]
        return block.reshape(parts * block.shape[1], block.shape[2])

    def drain(self):
        self.y.drain()
        for j in range(1, self.n):
            self.out_copy(j).wait_send()
            self.back_copy(j).wait_send()


def layer_kernel(
    scale, x_ref, wq_ref, wk_ref, wv_ref, gate_ref, cot_ref, blended_ref, out_ref,
    x_all, w_all, cot, kvq, prev, halo_out, halo_in, own_grads, dq_att, local_out,
    scores, soft_grads, grad_local, grad_num, den, grads, g_all,
    n1_own, n1_got, n1_yown, n1_ygot, n2_own, n2_got, n2_yown, n2_ygot, norms,
    m1_parts, m1_got, m1_inside, m1_yown, m1_ygot, m1_back, m1_full,
    m2_parts, m2_got, m2_inside, m2_yown, m2_ygot, m2_back, m2_full,
    dw, a_sum, b_sum, fin, swap,
    a1_send, a1_recv, b1_send, b1_recv, a2_send, a2_recv, b2_send, b2_recv,
    local_sem, halo_sem, pair_sem, nz_sem, ny_sem, mz_sem, my_sem, mb_sem, z1_sem, y1_sem, y2_sem, z2_sem,
):
    ny, nz = lax.axis_size("y"), lax.axis_size("z")
    y, z, dp = lax.axis_index("y"), lax.axis_index("z"), lax.axis_index("dp")
    other = {"dp": 1 - dp}
    tokens = x_ref.shape[0]
    heads, dim = kvq.shape[0] // 3, kvq.shape[2]
    half = grads.shape[2] // 2
    wide = dw.shape[1]
    block = wide // nz
    rows = block // 2
    up, down = z == nz - 1, z == 0
    after = {
        "y": lax.rem(y + jnp.where(up, 1, 0), ny), "z": lax.rem(z + 1, nz),
    }
    ahead_of = {
        "y": lax.rem(y - jnp.where(down, 1, 0) + ny, ny), "z": lax.rem(z - 1 + nz, nz),
    }
    score_scale = dim ** (-0.5)

    barrier = pltpu.get_barrier_semaphore()
    partners = [other, after, ahead_of]
    partners += [{"z": lax.rem(z + j, nz)} for j in range(1, nz)]
    partners += [{"y": lax.rem(y + j, ny)} for j in range(1, ny)]
    for device in partners:
        pl.semaphore_signal(barrier, inc=1, device_id=device, device_id_type=MESH)

    x_in = pltpu.make_async_copy(x_ref, x_all.at[pl.ds(0, tokens)], local_sem.at[0])
    cot_in = pltpu.make_async_copy(cot_ref, cot, local_sem.at[1])
    w_in = [
        pltpu.make_async_copy(w.at[:, pl.ds(h * dim, dim)], w_all.at[at * heads + h], local_sem.at[2 + at * heads + h])
        for at, w in enumerate((wk_ref, wv_ref, wq_ref)) for h in range(heads)
    ]
    x_in.start()
    for copy in w_in:
        copy.start()
    cot_in.start()

    def project(at):
        for h in range(heads):
            w_in[at * heads + h].wait()
        def body(h, carry):
            c = at * heads + h
            kvq[c] = dot_nn(x_all[pl.ds(0, tokens), :], w_all[c]).astype(jnp.bfloat16)
            return carry
        lax.fori_loop(0, heads, body, 0)

    def halo_copy(src, dst, slot, device):
        return pltpu.make_async_remote_copy(
            src_ref=src.at[pl.ds((slot % 2) * heads, heads)], dst_ref=dst.at[pl.ds((slot % 2) * heads, heads)],
            send_sem=halo_sem.at[0, slot], recv_sem=halo_sem.at[1, slot],
            device_id=device, device_id_type=MESH,
        )

    def pair_copy(src, dst, slot):
        return pltpu.make_async_remote_copy(
            src_ref=src, dst_ref=dst, send_sem=pair_sem.at[0, slot], recv_sem=pair_sem.at[1, slot],
            device_id=other, device_id_type=MESH,
        )

    def each_head(body):
        def step(h, carry):
            body(h)
            return carry
        lax.fori_loop(0, heads, step, 0)

    def columns(h):
        return pl.ds(pl.multiple_of(h * dim, dim), dim)

    norm_scan = VectorScan(False, n1_own, n1_got, n1_yown, n1_ygot, nz_sem.at[0], ny_sem.at[0])
    grad_norm_scan = VectorScan(True, n2_own, n2_got, n2_yown, n2_ygot, nz_sem.at[1], ny_sem.at[1])
    memory_scan = MemoryScan(
        False, m1_parts, m1_got, m1_inside, m1_yown, m1_ygot, m1_back, m1_full,
        mz_sem.at[0], my_sem.at[0], mb_sem.at[0],
    )
    grad_memory_scan = MemoryScan(
        True, m2_parts, m2_got, m2_inside, m2_yown, m2_ygot, m2_back, m2_full,
        mz_sem.at[1], my_sem.at[1], mb_sem.at[1],
    )
    parts = nz // heads

    def put_parts(target, h, value):
        target[pl.ds(h * parts, parts)] = value.astype(jnp.bfloat16).reshape(parts, dim // parts, dim)

    x_in.wait()
    project(0)

    def key_sums(h):
        n1_own[h] = jnp.sum(feature(kvq[h].astype(jnp.float32)), axis=0, keepdims=True)

    each_head(key_sums)
    pl.semaphore_wait(barrier, len(partners))
    norm_scan.start()
    halo_keys = halo_copy(kvq, prev, 0, after)
    halo_keys.start()
    project(1)

    def write(h):
        phi = feature(kvq[h].astype(jnp.float32)).astype(jnp.bfloat16)
        put_parts(m1_parts, h, dot_tn(phi, kvq[heads + h]))

    each_head(write)
    memory_scan.start()
    halo_values = halo_copy(kvq, prev, 1, after)
    halo_values.start()
    x_out = pair_copy(x_all.at[pl.ds(0, tokens)], x_all.at[pl.ds(tokens, tokens)], 0)
    x_out.start()
    project(2)
    cot_in.wait()
    norm_scan.across_rows()

    def own_part(h):
        query = kvq[2 * heads + h]
        mixing = 1.0 / (1.0 + jnp.exp(-jnp.full((1, dim), gate_ref[h], jnp.float32)))
        upstream = cot[:, columns(h)].astype(jnp.float32)
        local = ((1.0 - mixing) * upstream).astype(jnp.bfloat16)
        grad_local[h] = local
        row = lax.broadcasted_iota(jnp.int32, (tokens, tokens), 0)
        col = lax.broadcasted_iota(jnp.int32, (tokens, tokens), 1)
        scores[h] = jnp.where(col <= row, dot_nt(query, kvq[h]) * score_scale, MASKED)
        soft_grads[h] = dot_nt(local, kvq[heads + h])

    each_head(own_part)
    norms[...] = norm_scan.result()

    def memory_gradient(h):
        mixing = 1.0 / (1.0 + jnp.exp(-jnp.full((1, dim), gate_ref[h], jnp.float32)))
        phi = feature(kvq[2 * heads + h].astype(jnp.float32))
        divisor = jnp.sum(phi * norms[h], axis=1, keepdims=True) + 1.0
        den[h] = divisor
        grad_ret = mixing * cot[:, columns(h)].astype(jnp.float32)
        number = (grad_ret / divisor).astype(jnp.bfloat16)
        grad_num[h] = number
        put_parts(m2_parts, h, dot_tn(phi.astype(jnp.bfloat16), number))

    each_head(memory_gradient)
    grad_memory_scan.start()
    memory_scan.across_rows()

    bias = jnp.where(y * nz + z > 0, 0.0, MASKED)
    halo_keys.wait_recv()
    halo_values.wait_recv()
    memory_scan.give_back()

    def attend(h):
        query, key, value = kvq[2 * heads + h], kvq[h], kvq[heads + h]
        key_prev, value_prev, local = prev[h], prev[heads + h], grad_local[h]
        s_own = scores[h]
        s_prev = dot_nt(query, key_prev) * score_scale + bias
        top = jnp.maximum(jnp.max(s_own, axis=1, keepdims=True), jnp.max(s_prev, axis=1, keepdims=True))
        e_own, e_prev = jnp.exp(s_own - top), jnp.exp(s_prev - top)
        inverse = 1.0 / (jnp.sum(e_own, axis=1, keepdims=True) + jnp.sum(e_prev, axis=1, keepdims=True))
        p_own, p_prev = e_own * inverse, e_prev * inverse
        b_own, b_prev = p_own.astype(jnp.bfloat16), p_prev.astype(jnp.bfloat16)
        local_out[h] = dot_nn(b_own, value) + dot_nn(b_prev, value_prev)
        g_own, g_prev = soft_grads[h], dot_nt(local, value_prev)
        row_dot = jnp.sum(p_own * g_own, axis=1, keepdims=True) + jnp.sum(p_prev * g_prev, axis=1, keepdims=True)
        d_own = (p_own * (g_own - row_dot) * score_scale).astype(jnp.bfloat16)
        d_prev = (p_prev * (g_prev - row_dot) * score_scale).astype(jnp.bfloat16)
        halo_out[h] = dot_tn(d_prev, query).astype(jnp.bfloat16)
        halo_out[heads + h] = dot_tn(b_prev, local).astype(jnp.bfloat16)
        own_grads[h] = dot_tn(d_own, query)
        own_grads[heads + h] = dot_tn(b_own, local)
        dq_att[h] = dot_nn(d_own, key) + dot_nn(d_prev, key_prev)

    each_head(attend)
    back_keys, back_values = (halo_copy(halo_out, halo_in, slot, ahead_of) for slot in (2, 3))
    back_keys.start()
    back_values.start()
    grad_memory_scan.across_rows()
    memory_scan.finish()

    def retrieve(h):
        mixing = 1.0 / (1.0 + jnp.exp(-jnp.full((1, dim), gate_ref[h], jnp.float32)))
        query = kvq[2 * heads + h].astype(jnp.float32)
        phi = feature(query)
        memory = memory_scan.head(h, heads)
        retrieved = dot_nn(phi.astype(jnp.bfloat16), memory) / den[h]
        blended_ref[:, columns(h)] = (mixing * retrieved + (1.0 - mixing) * local_out[h]).astype(jnp.bfloat16)
        grad_ret = mixing * cot[:, columns(h)].astype(jnp.float32)
        grad_den = -jnp.sum(grad_ret * retrieved, axis=1, keepdims=True) / den[h]
        n2_own[h] = jnp.sum(grad_den * phi, axis=0, keepdims=True)
        grad_phi = dot_nt(grad_num[h], memory) + grad_den * norms[h]
        grads[h, :, :dim] = (dq_att[h] + grad_phi * feature_slope(query)).astype(jnp.bfloat16)

    each_head(retrieve)
    grad_norm_scan.start()
    grad_memory_scan.give_back()
    grad_norm_scan.across_rows()
    norms[...] = grad_norm_scan.result()
    back_keys.wait_recv()
    back_values.wait_recv()
    grad_memory_scan.finish()

    def write_back(h):
        key = kvq[h].astype(jnp.float32)
        grad_memory = grad_memory_scan.head(h, heads)
        grad_phi = dot_nt(kvq[heads + h], grad_memory) + norms[h]
        grad_key = own_grads[h] + halo_in[h].astype(jnp.float32) + grad_phi * feature_slope(key)
        grads[h, :, dim:2 * dim] = grad_key.astype(jnp.bfloat16)
        grad_value = dot_nn(feature(key).astype(jnp.bfloat16), grad_memory)
        grad_value = own_grads[heads + h] + halo_in[heads + h].astype(jnp.float32) + grad_value
        grads[h, :, 2 * dim:] = grad_value.astype(jnp.bfloat16)

    each_head(write_back)

    g_out = pair_copy(grads.at[1 - dp], g_all.at[pl.ds(tokens, tokens)], 1)
    g_out.start()
    g_all[pl.ds(0, tokens), :] = grads[dp]
    x_out.wait_recv()
    g_out.wait_recv()
    tile = min(wide, 256)

    def products(target):
        def body(i, carry):
            start = pl.multiple_of(target * wide + i * tile, 128)
            dw[target, pl.ds(pl.multiple_of(i * tile, 8), tile), :] = dot_tn(x_all[:, pl.ds(start, tile)], g_all[...])
            return carry
        lax.fori_loop(0, wide // tile, body, 0)

    def a1_mine(target, sub):
        return dw[:, pl.ds(pl.multiple_of(target * block + sub * rows, 8), rows), :half]

    def b1_mine(target, sub):
        return dw[target, sub * (wide // 2):(sub + 1) * (wide // 2), half:]

    def b2_mine(target, sub):
        return b_sum[pl.ds(pl.multiple_of(target * block + sub * rows, 8), rows), :]

    a1 = RingSum("z", a1_mine, a1_send, a1_recv, z1_sem.at[0], z1_sem.at[1])
    b1 = RingSum("y", b1_mine, b1_send, b1_recv, y1_sem.at[0], y1_sem.at[1])
    a2 = RingSum("y", lambda k, sub: a_sum[sub, k], a2_send, a2_recv, y2_sem.at[0], y2_sem.at[1])
    b2 = RingSum("z", b2_mine, b2_send, b2_recv, z2_sem.at[0], z2_sem.at[1])

    for step in range(ny):
        ahead = ny // 2 - step
        products(lax.rem(y + ahead + ny, ny))
        b1.step(0, ahead)
    a1.step(0)
    a1.step(1)
    b1.step(1)
    for t in range(2, nz // 2):
        a1.step(t)
    for sub in (0, 1):
        b_sum[sub * (wide // 2):(sub + 1) * (wide // 2), :] = b1.total(sub)
    b2.step(0)
    for sub in (0, 1):
        a_sum[sub] = a1.total(sub)
    for t in range(max(ny, nz) // 2):
        a2.step(t)
        b2.step(t + 1)
    for sub in (0, 1):
        fin[sub, :, :half] = a2.total(sub) * scale
        fin[sub, :, half:] = b2.total(sub) * scale
    swap_out = pair_copy(fin.at[1 - dp], swap, 2)
    swap_out.start()
    out_ref[dp] = fin[dp]
    for sent in (
        a1, b1, a2, b2, norm_scan, grad_norm_scan, memory_scan, grad_memory_scan,
    ):
        sent.drain()
    for copy in (halo_keys, halo_values, back_keys, back_values, x_out, g_out):
        copy.wait_send()
    swap_out.wait()
    out_ref[1 - dp] = swap[...]


def layer(x, wq, wk, wv, gate, cot, scale):
    tokens, depth = x.shape
    heads = gate.shape[0]
    dim = wq.shape[1] // heads
    cols = 3 * dim
    ny, nz = lax.axis_size("y"), lax.axis_size("z")
    wide = depth // ny
    rows = wide // nz // 2
    half = cols // 2
    zs, ys = 2 * (nz - 1), 2 * (ny - 1)
    wire = lambda *shape: pltpu.VMEM(shape, jnp.bfloat16)
    real = lambda *shape: pltpu.VMEM(shape, jnp.float32)
    dma = lambda *shape: pltpu.SemaphoreType.DMA(shape)
    a1, b1, last = (zs, ny, rows, half), (ys, wide // 2, half), (rows, half)
    part = (heads * dim // nz, dim)
    vectors = [real(heads, 1, dim), real(nz, heads, 1, dim), real(heads, 1, dim), real(ny, heads, 1, dim)]
    scan = [
        wire(nz, *part), wire(nz, *part), real(nz, *part), real(*part), real(ny, *part), wire(nz, *part),
        wire(nz, *part),
    ]
    pair = (2 * heads, tokens, dim)
    anywhere = pl.BlockSpec(memory_space=pl.ANY)
    return pl.pallas_call(
        functools.partial(layer_kernel, scale),
        out_shape=(
            jax.ShapeDtypeStruct((tokens, heads * dim), jnp.bfloat16),
            jax.ShapeDtypeStruct((2, rows, cols), jnp.float32),
        ),
        in_specs=[anywhere] * 4 + [pl.BlockSpec(memory_space=pltpu.SMEM), anywhere],
        out_specs=(pl.BlockSpec(memory_space=pltpu.VMEM),) * 2,
        scratch_shapes=[
            wire(2 * tokens, depth), wire(3 * heads, depth, dim), wire(tokens, heads * dim),
            wire(3 * heads, tokens, dim), wire(*pair), wire(*pair), wire(*pair), real(*pair),
            real(heads, tokens, dim), real(heads, tokens, dim),
            real(heads, tokens, tokens), real(heads, tokens, tokens), wire(heads, tokens, dim),
            wire(heads, tokens, dim), real(heads, tokens, 1), wire(heads, tokens, cols), wire(2 * tokens, cols),
            *vectors, *vectors, real(heads, 1, dim), *scan, *scan,
            real(ny, wide, cols), real(2, ny, rows, half), real(wide, half), real(2, rows, cols), real(rows, cols),
            wire(*a1), wire(*a1), wire(*b1), wire(*b1),
            wire(ys, *last), wire(ys, *last), wire(zs, *last), wire(zs, *last),
            dma(2 + 3 * heads), dma(2, 4), dma(2, 3), dma(2, 2, nz), dma(2, 2, ny),
            dma(2, 2, nz), dma(2, 2, ny), dma(2, 2, nz), dma(2, zs), dma(2, ys), dma(2, ys), dma(2, zs),
        ],
        compiler_params=pltpu.CompilerParams(
            collective_id=1, has_side_effects=True, vmem_limit_bytes=63 * 1024 * 1024
        ),
    )(x, wq, wk, wv, gate, cot)


def local(inputs, w_query, w_key, w_value, gate_bias, cotangent):
    tokens = inputs[0]
    seg_len = tokens.shape[0]
    columns = w_query.shape[1]
    head_dim = columns // gate_bias.shape[0]
    scale = 1.0 / math.sqrt(lax.axis_size(SEQ) * lax.axis_size("dp") * seg_len)
    blended, summed = layer(tokens, w_query, w_key, w_value, gate_bias, cotangent[0], scale)
    rows = summed.shape[1]
    grad_weights = summed.reshape(2, rows, 3, head_dim).transpose(1, 2, 0, 3).reshape(rows, 3, columns)
    return (blended[None], grad_weights)


def solution(mesh):
    finer = Mesh(
        mesh.devices.reshape(4, 8, mesh.shape["dp"], mesh.shape["head"]),
        ("y", "z", "dp", "head"),
    )
    placed = (
        P("dp", SEQ, None),
        P(None, "head"),
        P(None, "head"),
        P(None, "head"),
        P("head"),
        P("dp", SEQ, "head"),
    )
    return jax.shard_map(
        local,
        mesh=finer,
        in_specs=placed,
        out_specs=(P("dp", SEQ, "head"), P(SEQ_DP, None, "head")),
        check_vma=False,
    )
```

time: 311 us -> 124 us (0.40)
  blocking collectives: 73.5 us -> 0 us
  Pallas kernels: 59.8 us -> 119 us
  matrix products: 54 us -> 0 us
  waiting for transfers between devices: 53.3 us -> 0 us
  local copies, waits for them, and re-layouts: 29.8 us -> 4.06 us
  other arithmetic: 21.6 us -> 0 us
  between operations: 14.1 us -> 0.65 us
  starting transfers between devices: 3.8 us -> 0 us
    all_gather x4 -> x0, blocking collectives: 73.5 us -> none  [prefix_by_axis(): pieces = jax.tree.map(lambda part: lax.all_gather(part, axis), subtotal)]
    pallas_call x1, Pallas kernels: 59.8 us -> 119 us  [layer(): pl.pallas_call(functools.partial(layer_kernel, scale), out_shape=(jax.Sha...]
    dot_general x16 -> x0, matrix products: 49.6 us -> none  [the longest x5 27.8 us: product(): return jnp.einsum(form, left, right, preferred_element_type=jnp.float32)]
    ppermute x2 -> x0, waiting for transfers between devices: 36.4 us -> none  [passed_along(): return lax.ppermute(x, axis, pairs)]
    all_gather x4 -> x0, waiting for transfers between devices: 16.8 us -> none  [prefix_by_axis(): pieces = jax.tree.map(lambda part: lax.all_gather(part, axis), subtotal)]
    add x10 -> x0, other arithmetic: 13.3 us -> none  [the longest x7 13.3 us: add_pair(): return (earlier[0] + latter[0], earlier[1] + latter[1])]
    another operation x4 -> x0, local copies, waits for them, and re-layouts: 6.17 us -> none  [the longest x2 2.36 us: local(): jnp.stack([grad_keys[:seg_len], grad_values[:seg_len]]).astype(jnp.bfloat16)]
    convert_element_type x3 -> x0, local copies, waits for them, and re-layouts: 5.91 us -> none  [the longest x2 3.85 us: project(): jnp.dot(tokens, weight, preferred_element_type=jnp.float32)]
  transfers between devices with their start and end apart: 6 -> 0, of which waited for: 5 -> 0; matrix products, arithmetic and copies ran while one was open for 25% -> 0% of each run, Pallas kernels for 0% -> 0%
where the time goes in v2:
time: 124 us
  Pallas kernels  119 us (96%)
  local copies, waits for them, and re-layouts  4.06 us (3%)
    pallas_call x1, Pallas kernels, layer(): pl.pallas_call(functools.partial(layer_kernel, scale), out_shape=(jax.Sha...  119 us

profile of v2, /device:TPU:1, one launch (start us, length us, event | category | flops | bytes accessed | tf_op | source)
XLA Modules:
  0.0 124.2 jit_solution(3994681833383040884)
XLA Ops:
  0.6 119.5 %shard_map.77 = (bf16[384,512]{1,0:T(8,128)(2,1)}, f32[2,48,768]{2,1,0:T(8,128)}) custom-call(bf16[384,3072]{1,0:T(8,128)(2,1)} %bitcast.6, bf16[3072,512]{1,0:T(8,128)(2,1)} %wq_ref.1, bf16[3072,512]{1,0:T(8,128)(2,1)} %wk_ref.1, bf16[3072,512]{1,0:T(8,128)(2,1)} %wv_ref.1, f32[2]{0:T(128)} %gate_ref.1, bf16[384,512]{1,0:T(8,128)(2,1)} %bitcast.8), custom_call_target="tpu_custom_call" | custom-call | tf_op jit(solution)/shard_map/pallas_call | solution.py:522
  120.1 1.1 reshape.10
  121.2 0.2 copy.9
  121.5 1.0 reshape.11
  122.4 1.8 %copy.11 = bf16[1,384,512]{2,1,0:T(8,128)(2,1)} copy(bf16[1,384,512]{2,1,0:T(8,128)(2,1)} %bitcast.9) | data formatting | bytes 786432

commit v3 on v2

--- a/solution.py
+++ b/solution.py
@@ -223,22 +223,21 @@
 
 def layer_kernel(
     scale, x_ref, wq_ref, wk_ref, wv_ref, gate_ref, cot_ref, blended_ref, out_ref,
-    x_all, w_all, cot, kvq, prev, halo_out, halo_in, own_grads, dq_att, local_out,
-    scores, soft_grads, grad_local, grad_num, den, grads, g_all,
+    x_all, w_all, cot, kvq, prev, after_in, own_grads, dq_ret, ret_mix,
+    scores, soft_grads, grad_local, grad_num, den, stats, stats_in, grads, g_all,
     n1_own, n1_got, n1_yown, n1_ygot, n2_own, n2_got, n2_yown, n2_ygot, norms,
     m1_parts, m1_got, m1_inside, m1_yown, m1_ygot, m1_back, m1_full,
     m2_parts, m2_got, m2_inside, m2_yown, m2_ygot, m2_back, m2_full,
-    dw, a_sum, b_sum, fin, swap,
-    a1_send, a1_recv, b1_send, b1_recv, a2_send, a2_recv, b2_send, b2_recv,
-    local_sem, halo_sem, pair_sem, nz_sem, ny_sem, mz_sem, my_sem, mb_sem, z1_sem, y1_sem, y2_sem, z2_sem,
+    dw, a_sum, b_sum, q_sum, fin, swap,
+    a1_send, a1_recv, b1_send, b1_recv, q1_send, q1_recv, a2_send, a2_recv, b2_send, b2_recv, q2_send, q2_recv,
+    local_sem, halo_sem, pair_sem, nz_sem, ny_sem, mz_sem, my_sem, mb_sem, z1_sem, y1_sem, yq_sem, y2_sem, z2_sem, zq_sem,
 ):
     ny, nz = lax.axis_size("y"), lax.axis_size("z")
     y, z, dp = lax.axis_index("y"), lax.axis_index("z"), lax.axis_index("dp")
     other = {"dp": 1 - dp}
     tokens = x_ref.shape[0]
     heads, dim = kvq.shape[0] // 3, kvq.shape[2]
-    half = grads.shape[2] // 2
-    wide = dw.shape[1]
+    wide = dw.shape[2]
     block = wide // nz
     rows = block // 2
     up, down = z == nz - 1, z == 0
@@ -264,9 +263,11 @@
         for at, w in enumerate((wk_ref, wv_ref, wq_ref)) for h in range(heads)
     ]
     x_in.start()
-    for copy in w_in:
+    for copy in w_in[:heads]:
         copy.start()
     cot_in.start()
+    for copy in w_in[heads:]:
+        copy.start()
 
     def project(at):
         for h in range(heads):
@@ -279,10 +280,17 @@
 
     def halo_copy(src, dst, slot, device):
         return pltpu.make_async_remote_copy(
-            src_ref=src.at[pl.ds((slot % 2) * heads, heads)], dst_ref=dst.at[pl.ds((slot % 2) * heads, heads)],
-            send_sem=halo_sem.at[0, slot], recv_sem=halo_sem.at[1, slot],
+            src_ref=src, dst_ref=dst, send_sem=halo_sem.at[0, slot], recv_sem=halo_sem.at[1, slot],
             device_id=device, device_id_type=MESH,
         )
+
+    key_out = [halo_copy(kvq.at[h], prev.at[h], h, after) for h in range(heads)]
+    value_out = halo_copy(kvq.at[pl.ds(heads, heads)], prev.at[pl.ds(heads, heads)], heads, after)
+    local_out = [
+        halo_copy(grad_local.at[h], after_in.at[heads + h], heads + 1 + h, ahead_of) for h in range(heads)
+    ]
+    query_out = halo_copy(kvq.at[pl.ds(2 * heads, heads)], after_in.at[pl.ds(0, heads)], 2 * heads + 1, ahead_of)
+    stats_out = halo_copy(stats, stats_in, 2 * heads + 2, ahead_of)
 
     def pair_copy(src, dst, slot):
         return pltpu.make_async_remote_copy(
@@ -314,6 +322,9 @@
     def put_parts(target, h, value):
         target[pl.ds(h * parts, parts)] = value.astype(jnp.bfloat16).reshape(parts, dim // parts, dim)
 
+    def mixing_of(h):
+        return 1.0 / (1.0 + jnp.exp(-jnp.full((1, dim), gate_ref[h], jnp.float32)))
+
     x_in.wait()
     project(0)
 
@@ -321,10 +332,19 @@
         n1_own[h] = jnp.sum(feature(kvq[h].astype(jnp.float32)), axis=0, keepdims=True)
 
     each_head(key_sums)
+    cot_in.wait()
+
+    def local_gradient(h):
+        upstream = cot[:, columns(h)].astype(jnp.float32)
+        grad_local[h] = ((1.0 - mixing_of(h)) * upstream).astype(jnp.bfloat16)
+
+    each_head(local_gradient)
     pl.semaphore_wait(barrier, len(partners))
     norm_scan.start()
-    halo_keys = halo_copy(kvq, prev, 0, after)
-    halo_keys.start()
+    key_out[0].start()
+    local_out[0].start()
+    x_out = pair_copy(x_all.at[pl.ds(0, tokens)], x_all.at[pl.ds(tokens, tokens)], 0)
+    x_out.start()
     project(1)
 
     def write(h):
@@ -333,46 +353,77 @@
 
     each_head(write)
     memory_scan.start()
-    halo_values = halo_copy(kvq, prev, 1, after)
-    halo_values.start()
-    x_out = pair_copy(x_all.at[pl.ds(0, tokens)], x_all.at[pl.ds(tokens, tokens)], 0)
-    x_out.start()
     project(2)
-    cot_in.wait()
     norm_scan.across_rows()
 
     def own_part(h):
-        query = kvq[2 * heads + h]
-        mixing = 1.0 / (1.0 + jnp.exp(-jnp.full((1, dim), gate_ref[h], jnp.float32)))
-        upstream = cot[:, columns(h)].astype(jnp.float32)
-        local = ((1.0 - mixing) * upstream).astype(jnp.bfloat16)
-        grad_local[h] = local
         row = lax.broadcasted_iota(jnp.int32, (tokens, tokens), 0)
         col = lax.broadcasted_iota(jnp.int32, (tokens, tokens), 1)
-        scores[h] = jnp.where(col <= row, dot_nt(query, kvq[h]) * score_scale, MASKED)
-        soft_grads[h] = dot_nt(local, kvq[heads + h])
+        scores[h] = jnp.where(col <= row, dot_nt(kvq[2 * heads + h], kvq[h]) * score_scale, MASKED)
+        soft_grads[h] = dot_nt(grad_local[h], kvq[heads + h])
 
     each_head(own_part)
-    norms[...] = norm_scan.result()
+    norms[0] = norm_scan.result()
 
     def memory_gradient(h):
-        mixing = 1.0 / (1.0 + jnp.exp(-jnp.full((1, dim), gate_ref[h], jnp.float32)))
         phi = feature(kvq[2 * heads + h].astype(jnp.float32))
-        divisor = jnp.sum(phi * norms[h], axis=1, keepdims=True) + 1.0
+        divisor = jnp.sum(phi * norms[0, h], axis=1, keepdims=True) + 1.0
         den[h] = divisor
-        grad_ret = mixing * cot[:, columns(h)].astype(jnp.float32)
+        grad_ret = mixing_of(h) * cot[:, columns(h)].astype(jnp.float32)
         number = (grad_ret / divisor).astype(jnp.bfloat16)
         grad_num[h] = number
         put_parts(m2_parts, h, dot_tn(phi.astype(jnp.bfloat16), number))
 
     each_head(memory_gradient)
     grad_memory_scan.start()
+    for h in range(1, heads):
+        key_out[h].start()
+        local_out[h].start()
     memory_scan.across_rows()
-
-    bias = jnp.where(y * nz + z > 0, 0.0, MASKED)
-    halo_keys.wait_recv()
-    halo_values.wait_recv()
     memory_scan.give_back()
+    value_out.start()
+    query_out.start()
+    grad_memory_scan.across_rows()
+
+    x_out.wait_recv()
+    spans = 2 * tokens // dim
+    tile = min(wide, 256)
+
+    def turn(i, carry):
+        at = pl.ds(pl.multiple_of(i * tile, 128), tile)
+        for c in range(spans):
+            w_all[c, at, :] = x_all[c * dim:(c + 1) * dim, at].T
+        return carry
+
+    lax.fori_loop(0, x_all.shape[1] // tile, turn, 0)
+    memory_scan.finish()
+
+    def retrieve(h):
+        mixing = mixing_of(h)
+        query = kvq[2 * heads + h].astype(jnp.float32)
+        phi = feature(query)
+        memory = memory_scan.head(h, heads)
+        retrieved = dot_nn(phi.astype(jnp.bfloat16), memory) / den[h]
+        ret_mix[h] = mixing * retrieved
+        grad_ret = mixing * cot[:, columns(h)].astype(jnp.float32)
+        grad_den = -jnp.sum(grad_ret * retrieved, axis=1, keepdims=True) / den[h]
+        n2_own[h] = jnp.sum(grad_den * phi, axis=0, keepdims=True)
+        grad_phi = dot_nt(grad_num[h], memory) + grad_den * norms[0, h]
+        dq_ret[h] = grad_phi * feature_slope(query)
+
+    each_head(retrieve)
+    grad_norm_scan.start()
+    grad_memory_scan.give_back()
+
+    segment, last = y * nz + z, ny * nz - 1
+    bias = jnp.where(segment > 0, 0.0, MASKED)
+    bias_after = jnp.where(segment < last, 0.0, MASKED)
+    for copy in key_out:
+        copy.wait_recv()
+    value_out.wait_recv()
+
+    def as_row(column):
+        return jnp.broadcast_to(column, (tokens, 128)).T[:1]
 
     def attend(h):
         query, key, value = kvq[2 * heads + h], kvq[h], kvq[heads + h]
@@ -384,133 +435,160 @@
         inverse = 1.0 / (jnp.sum(e_own, axis=1, keepdims=True) + jnp.sum(e_prev, axis=1, keepdims=True))
         p_own, p_prev = e_own * inverse, e_prev * inverse
         b_own, b_prev = p_own.astype(jnp.bfloat16), p_prev.astype(jnp.bfloat16)
-        local_out[h] = dot_nn(b_own, value) + dot_nn(b_prev, value_prev)
+        near = dot_nn(b_own, value) + dot_nn(b_prev, value_prev)
+        blended_ref[:, columns(h)] = (ret_mix[h] + (1.0 - mixing_of(h)) * near).astype(jnp.bfloat16)
         g_own, g_prev = soft_grads[h], dot_nt(local, value_prev)
         row_dot = jnp.sum(p_own * g_own, axis=1, keepdims=True) + jnp.sum(p_prev * g_prev, axis=1, keepdims=True)
+        stats[h, 0:1] = as_row(top)
+        stats[h, 1:2] = as_row(inverse)
+        stats[h, 2:3] = as_row(row_dot)
         d_own = (p_own * (g_own - row_dot) * score_scale).astype(jnp.bfloat16)
         d_prev = (p_prev * (g_prev - row_dot) * score_scale).astype(jnp.bfloat16)
-        halo_out[h] = dot_tn(d_prev, query).astype(jnp.bfloat16)
-        halo_out[heads + h] = dot_tn(b_prev, local).astype(jnp.bfloat16)
         own_grads[h] = dot_tn(d_own, query)
         own_grads[heads + h] = dot_tn(b_own, local)
-        dq_att[h] = dot_nn(d_own, key) + dot_nn(d_prev, key_prev)
-
+        dq_att = dot_nn(d_own, key) + dot_nn(d_prev, key_prev)
+        grads[0, h] = (dq_att + dq_ret[h]).astype(jnp.bfloat16)
+
+    for h in range(heads):
+        stats[h] = jnp.zeros(stats.shape[1:], jnp.float32)
     each_head(attend)
-    back_keys, back_values = (halo_copy(halo_out, halo_in, slot, ahead_of) for slot in (2, 3))
-    back_keys.start()
-    back_values.start()
-    grad_memory_scan.across_rows()
-    memory_scan.finish()
-
-    def retrieve(h):
-        mixing = 1.0 / (1.0 + jnp.exp(-jnp.full((1, dim), gate_ref[h], jnp.float32)))
-        query = kvq[2 * heads + h].astype(jnp.float32)
-        phi = feature(query)
-        memory = memory_scan.head(h, heads)
-        retrieved = dot_nn(phi.astype(jnp.bfloat16), memory) / den[h]
-        blended_ref[:, columns(h)] = (mixing * retrieved + (1.0 - mixing) * local_out[h]).astype(jnp.bfloat16)
-        grad_ret = mixing * cot[:, columns(h)].astype(jnp.float32)
-        grad_den = -jnp.sum(grad_ret * retrieved, axis=1, keepdims=True) / den[h]
-        n2_own[h] = jnp.sum(grad_den * phi, axis=0, keepdims=True)
-        grad_phi = dot_nt(grad_num[h], memory) + grad_den * norms[h]
-        grads[h, :, :dim] = (dq_att[h] + grad_phi * feature_slope(query)).astype(jnp.bfloat16)
-
-    each_head(retrieve)
-    grad_norm_scan.start()
-    grad_memory_scan.give_back()
+    stats_out.start()
+
+    def pair_grads(m):
+        return pair_copy(grads.at[m, 1 - dp], g_all.at[m, pl.ds(tokens, tokens)], 1 + m)
+
+    def keep_grads(m):
+        g_all[m, pl.ds(0, tokens), :] = grads[m, dp]
+
+    def products(m, target):
+        def body(i, carry):
+            at = pl.multiple_of(target * wide + i * tile, 128)
+            total = dot_nn(w_all[0, pl.ds(at, tile), :], g_all[m, 0:dim, :])
+            for c in range(1, spans):
+                total = total + dot_nn(w_all[c, pl.ds(at, tile), :], g_all[m, c * dim:(c + 1) * dim, :])
+            dw[m, target, pl.ds(pl.multiple_of(i * tile, 8), tile), :] = total
+            return carry
+        lax.fori_loop(0, wide // tile, body, 0)
+
+    def a1_mine(target, sub):
+        return dw[1, :, pl.ds(pl.multiple_of(target * block + sub * rows, 8), rows), :]
+
+    def y_first(m):
+        return lambda target, sub: dw[m, target, sub * (wide // 2):(sub + 1) * (wide // 2), :]
+
+    def z_second(held):
+        return lambda target, sub: held[pl.ds(pl.multiple_of(target * block + sub * rows, 8), rows), :]
+
+    a1 = RingSum("z", a1_mine, a1_send, a1_recv, z1_sem.at[0], z1_sem.at[1])
+    b1 = RingSum("y", y_first(2), b1_send, b1_recv, y1_sem.at[0], y1_sem.at[1])
+    q1 = RingSum("y", y_first(0), q1_send, q1_recv, yq_sem.at[0], yq_sem.at[1])
+    a2 = RingSum("y", lambda k, sub: a_sum[sub, k], a2_send, a2_recv, y2_sem.at[0], y2_sem.at[1])
+    b2 = RingSum("z", z_second(b_sum), b2_send, b2_recv, z2_sem.at[0], z2_sem.at[1])
+    q2 = RingSum("z", z_second(q_sum), q2_send, q2_recv, zq_sem.at[0], zq_sem.at[1])
+
+    def rows_in(ring, held):
+        for sub in (0, 1):
+            held[sub * (wide // 2):(sub + 1) * (wide // 2), :] = ring.total(sub)
+
+    query_pair = pair_grads(0)
+    query_pair.start()
+    keep_grads(0)
     grad_norm_scan.across_rows()
-    norms[...] = grad_norm_scan.result()
-    back_keys.wait_recv()
-    back_values.wait_recv()
+    query_pair.wait_recv()
+    for step in range(ny):
+        ahead = ny // 2 - step
+        products(0, lax.rem(y + ahead + ny, ny))
+        q1.step(0, ahead)
+
+    for copy in local_out:
+        copy.wait_recv()
+    query_out.wait_recv()
+    stats_out.wait_recv()
+
+    def serve(h):
+        query, local = after_in[h], after_in[heads + h]
+        top, inverse, row_dot = stats_in[h, 0:1], stats_in[h, 1:2], stats_in[h, 2:3]
+        soft = jnp.exp(dot_nt(kvq[h], query) * score_scale + bias_after - top) * inverse
+        given = (soft * (dot_nt(kvq[heads + h], local) - row_dot) * score_scale).astype(jnp.bfloat16)
+        own_grads[h] += dot_nn(given, query)
+        own_grads[heads + h] += dot_nn(soft.astype(jnp.bfloat16), local)
+
+    each_head(serve)
+    norms[1] = grad_norm_scan.result()
     grad_memory_scan.finish()
 
     def write_back(h):
         key = kvq[h].astype(jnp.float32)
         grad_memory = grad_memory_scan.head(h, heads)
-        grad_phi = dot_nt(kvq[heads + h], grad_memory) + norms[h]
-        grad_key = own_grads[h] + halo_in[h].astype(jnp.float32) + grad_phi * feature_slope(key)
-        grads[h, :, dim:2 * dim] = grad_key.astype(jnp.bfloat16)
+        grad_phi = dot_nt(kvq[heads + h], grad_memory) + norms[1, h]
+        grads[1, h] = (own_grads[h] + grad_phi * feature_slope(key)).astype(jnp.bfloat16)
         grad_value = dot_nn(feature(key).astype(jnp.bfloat16), grad_memory)
-        grad_value = own_grads[heads + h] + halo_in[heads + h].astype(jnp.float32) + grad_value
-        grads[h, :, 2 * dim:] = grad_value.astype(jnp.bfloat16)
+        grads[2, h] = (own_grads[heads + h] + grad_value).astype(jnp.bfloat16)
 
     each_head(write_back)
-
-    g_out = pair_copy(grads.at[1 - dp], g_all.at[pl.ds(tokens, tokens)], 1)
-    g_out.start()
-    g_all[pl.ds(0, tokens), :] = grads[dp]
-    x_out.wait_recv()
-    g_out.wait_recv()
-    tile = min(wide, 256)
-
-    def products(target):
-        def body(i, carry):
-            start = pl.multiple_of(target * wide + i * tile, 128)
-            dw[target, pl.ds(pl.multiple_of(i * tile, 8), tile), :] = dot_tn(x_all[:, pl.ds(start, tile)], g_all[...])
-            return carry
-        lax.fori_loop(0, wide // tile, body, 0)
-
-    def a1_mine(target, sub):
-        return dw[:, pl.ds(pl.multiple_of(target * block + sub * rows, 8), rows), :half]
-
-    def b1_mine(target, sub):
-        return dw[target, sub * (wide // 2):(sub + 1) * (wide // 2), half:]
-
-    def b2_mine(target, sub):
-        return b_sum[pl.ds(pl.multiple_of(target * block + sub * rows, 8), rows), :]
-
-    a1 = RingSum("z", a1_mine, a1_send, a1_recv, z1_sem.at[0], z1_sem.at[1])
-    b1 = RingSum("y", b1_mine, b1_send, b1_recv, y1_sem.at[0], y1_sem.at[1])
-    a2 = RingSum("y", lambda k, sub: a_sum[sub, k], a2_send, a2_recv, y2_sem.at[0], y2_sem.at[1])
-    b2 = RingSum("z", b2_mine, b2_send, b2_recv, z2_sem.at[0], z2_sem.at[1])
-
+    key_pair, value_pair = pair_grads(1), pair_grads(2)
+    key_pair.start()
+    value_pair.start()
+    keep_grads(1)
+    keep_grads(2)
+    key_pair.wait_recv()
+    for k in range(ny):
+        products(1, k)
+    a1.step(0)
+    value_pair.wait_recv()
     for step in range(ny):
         ahead = ny // 2 - step
-        products(lax.rem(y + ahead + ny, ny))
+        products(2, lax.rem(y + ahead + ny, ny))
         b1.step(0, ahead)
-    a1.step(0)
+    q1.step(1)
     a1.step(1)
+    rows_in(q1, q_sum)
+    q2.step(0)
+    a1.step(2)
     b1.step(1)
-    for t in range(2, nz // 2):
-        a1.step(t)
-    for sub in (0, 1):
-        b_sum[sub * (wide // 2):(sub + 1) * (wide // 2), :] = b1.total(sub)
+    q2.step(1)
+    a1.step(3)
+    q2.step(2)
+    rows_in(b1, b_sum)
     b2.step(0)
     for sub in (0, 1):
         a_sum[sub] = a1.total(sub)
-    for t in range(max(ny, nz) // 2):
-        a2.step(t)
-        b2.step(t + 1)
+    a2.step(0)
+    q2.step(3)
+    b2.step(1)
+    a2.step(1)
+    for t in range(2, nz // 2):
+        b2.step(t)
     for sub in (0, 1):
-        fin[sub, :, :half] = a2.total(sub) * scale
-        fin[sub, :, half:] = b2.total(sub) * scale
-    swap_out = pair_copy(fin.at[1 - dp], swap, 2)
+        for m, ring in enumerate((q2, a2, b2)):
+            fin[sub, :, m * dim:(m + 1) * dim] = ring.total(sub) * scale
+    swap_out = pair_copy(fin.at[1 - dp], swap, 4)
     swap_out.start()
-    out_ref[dp] = fin[dp]
+    for m in range(3):
+        out_ref[m, :, columns(dp)] = fin[dp, :, m * dim:(m + 1) * dim]
     for sent in (
-        a1, b1, a2, b2, norm_scan, grad_norm_scan, memory_scan, grad_memory_scan,
+        a1, b1, q1, a2, b2, q2, norm_scan, grad_norm_scan, memory_scan, grad_memory_scan,
     ):
         sent.drain()
-    for copy in (halo_keys, halo_values, back_keys, back_values, x_out, g_out):
+    for copy in (*key_out, value_out, *local_out, query_out, stats_out, x_out, query_pair, key_pair, value_pair):
         copy.wait_send()
     swap_out.wait()
-    out_ref[1 - dp] = swap[...]
+    for m in range(3):
+        out_ref[m, :, columns(1 - dp)] = swap[:, m * dim:(m + 1) * dim]
 
 
 def layer(x, wq, wk, wv, gate, cot, scale):
     tokens, depth = x.shape
     heads = gate.shape[0]
     dim = wq.shape[1] // heads
-    cols = 3 * dim
     ny, nz = lax.axis_size("y"), lax.axis_size("z")
     wide = depth // ny
     rows = wide // nz // 2
-    half = cols // 2
     zs, ys = 2 * (nz - 1), 2 * (ny - 1)
     wire = lambda *shape: pltpu.VMEM(shape, jnp.bfloat16)
     real = lambda *shape: pltpu.VMEM(shape, jnp.float32)
     dma = lambda *shape: pltpu.SemaphoreType.DMA(shape)
-    a1, b1, last = (zs, ny, rows, half), (ys, wide // 2, half), (rows, half)
+    a1, b1, last = (zs, ny, rows, dim), (ys, wide // 2, dim), (rows, dim)
     part = (heads * dim // nz, dim)
     vectors = [real(heads, 1, dim), real(nz, heads, 1, dim), real(heads, 1, dim), real(ny, heads, 1, dim)]
     scan = [
@@ -523,22 +601,25 @@
         functools.partial(layer_kernel, scale),
         out_shape=(
             jax.ShapeDtypeStruct((tokens, heads * dim), jnp.bfloat16),
-            jax.ShapeDtypeStruct((2, rows, cols), jnp.float32),
+            jax.ShapeDtypeStruct((3, rows, heads * dim), jnp.float32),
         ),
         in_specs=[anywhere] * 4 + [pl.BlockSpec(memory_space=pltpu.SMEM), anywhere],
         out_specs=(pl.BlockSpec(memory_space=pltpu.VMEM),) * 2,
         scratch_shapes=[
             wire(2 * tokens, depth), wire(3 * heads, depth, dim), wire(tokens, heads * dim),
-            wire(3 * heads, tokens, dim), wire(*pair), wire(*pair), wire(*pair), real(*pair),
+            wire(3 * heads, tokens, dim), wire(*pair), wire(*pair), real(*pair),
             real(heads, tokens, dim), real(heads, tokens, dim),
             real(heads, tokens, tokens), real(heads, tokens, tokens), wire(heads, tokens, dim),
-            wire(heads, tokens, dim), real(heads, tokens, 1), wire(heads, tokens, cols), wire(2 * tokens, cols),
-            *vectors, *vectors, real(heads, 1, dim), *scan, *scan,
-            real(ny, wide, cols), real(2, ny, rows, half), real(wide, half), real(2, rows, cols), real(rows, cols),
-            wire(*a1), wire(*a1), wire(*b1), wire(*b1),
-            wire(ys, *last), wire(ys, *last), wire(zs, *last), wire(zs, *last),
-            dma(2 + 3 * heads), dma(2, 4), dma(2, 3), dma(2, 2, nz), dma(2, 2, ny),
-            dma(2, 2, nz), dma(2, 2, ny), dma(2, 2, nz), dma(2, zs), dma(2, ys), dma(2, ys), dma(2, zs),
+            wire(heads, tokens, dim), real(heads, tokens, 1), real(heads, 8, tokens), real(heads, 8, tokens),
+            wire(3, heads, tokens, dim), wire(3, 2 * tokens, dim),
+            *vectors, *vectors, real(2, heads, 1, dim), *scan, *scan,
+            real(3, ny, wide, dim), real(2, ny, rows, dim), real(wide, dim), real(wide, dim),
+            real(2, rows, 3 * dim), real(rows, 3 * dim),
+            wire(*a1), wire(*a1), wire(*b1), wire(*b1), wire(*b1), wire(*b1),
+            wire(ys, *last), wire(ys, *last), wire(zs, *last), wire(zs, *last), wire(zs, *last), wire(zs, *last),
+            dma(2 + 3 * heads), dma(2, 2 * heads + 3), dma(2, 5), dma(2, 2, nz), dma(2, 2, ny),
+            dma(2, 2, nz), dma(2, 2, ny), dma(2, 2, nz),
+            dma(2, zs), dma(2, ys), dma(2, ys), dma(2, ys), dma(2, zs), dma(2, zs),
         ],
         compiler_params=pltpu.CompilerParams(
             collective_id=1, has_side_effects=True, vmem_limit_bytes=63 * 1024 * 1024
@@ -549,13 +630,9 @@
 def local(inputs, w_query, w_key, w_value, gate_bias, cotangent):
     tokens = inputs[0]
     seg_len = tokens.shape[0]
-    columns = w_query.shape[1]
-    head_dim = columns // gate_bias.shape[0]
     scale = 1.0 / math.sqrt(lax.axis_size(SEQ) * lax.axis_size("dp") * seg_len)
-    blended, summed = layer(tokens, w_query, w_key, w_value, gate_bias, cotangent[0], scale)
-    rows = summed.shape[1]
-    grad_weights = summed.reshape(2, rows, 3, head_dim).transpose(1, 2, 0, 3).reshape(rows, 3, columns)
-    return (blended[None], grad_weights)
+    blended, grad_weights = layer(tokens, w_query, w_key, w_value, gate_bias, cotangent[0], scale)
+    return (blended[None], grad_weights.transpose(1, 0, 2))
 
 
 def solution(mesh):

time: 124 us -> 111 us (0.90)
  Pallas kernels: 119 us -> 107 us
    pallas_call x1, Pallas kernels: 119 us -> 107 us  [layer(): pl.pallas_call(functools.partial(layer_kernel, scale), out_shape=(jax.Sha...]
    reshape x2 -> x0, local copies, waits for them, and re-layouts: 2.06 us -> none  [local(): summed.reshape(2, rows, 3, head_dim).transpose(1, 2, 0, 3)]
    unnamed x1 -> x2, local copies, waits for them, and re-layouts: 1.77 us -> 3.46 us
where the time goes in v3:
time: 111 us
  Pallas kernels  107 us (96%)
  local copies, waits for them, and re-layouts  3.46 us (3%)
    pallas_call x1, Pallas kernels, layer(): pl.pallas_call(functools.partial(layer_kernel, scale), out_shape=(jax.Sha...  107 us
    unnamed x2, local copies, waits for them, and re-layouts  3.46 us

profile of v3, /device:TPU:1, one launch (start us, length us, event | category | flops | bytes accessed | tf_op | source)
XLA Modules:
  0.0 110.7 jit_solution(8721308445557593448)
XLA Ops:
  0.6 106.6 %shard_map.77 = (bf16[384,512]{1,0:T(8,128)(2,1)}, f32[3,48,512]{2,1,0:T(8,128)}) custom-call(bf16[384,3072]{1,0:T(8,128)(2,1)} %bitcast.4, bf16[3072,512]{1,0:T(8,128)(2,1)} %wq_ref.1, bf16[3072,512]{1,0:T(8,128)(2,1)} %wk_ref.1, bf16[3072,512]{1,0:T(8,128)(2,1)} %wv_ref.1, f32[2]{0:T(128)} %gate_ref.1, bf16[384,512]{1,0:T(8,128)(2,1)} %bitcast.5), custom_call_target="tpu_custom_call" | custom-call | tf_op jit(solution)/shard_map/pallas_call | solution.py:600
  107.2 1.8 %copy.10 = bf16[1,384,512]{2,1,0:T(8,128)(2,1)} copy(bf16[1,384,512]{2,1,0:T(8,128)(2,1)} %bitcast.6) | data formatting | bytes 786432
  109.0 1.7 %copy.11 = f32[48,3,512]{2,0,1:T(8,128)} copy(f32[48,3,512]{2,0,1:T(8,128)} %bitcast.7) | data formatting | bytes 589824

commit v4 on v3

--- a/solution.py
+++ b/solution.py
@@ -223,14 +223,15 @@
 
 def layer_kernel(
     scale, x_ref, wq_ref, wk_ref, wv_ref, gate_ref, cot_ref, blended_ref, out_ref,
-    x_all, w_all, cot, kvq, prev, after_in, own_grads, dq_ret, ret_mix,
+    x_all, x_turned, w_all, cot, blended, kvq, prev, after_in, own_grads, dq_ret, ret_mix,
     scores, soft_grads, grad_local, grad_num, den, stats, stats_in, grads, g_all,
     n1_own, n1_got, n1_yown, n1_ygot, n2_own, n2_got, n2_yown, n2_ygot, norms,
     m1_parts, m1_got, m1_inside, m1_yown, m1_ygot, m1_back, m1_full,
     m2_parts, m2_got, m2_inside, m2_yown, m2_ygot, m2_back, m2_full,
-    dw, a_sum, b_sum, q_sum, fin, swap,
-    a1_send, a1_recv, b1_send, b1_recv, q1_send, q1_recv, a2_send, a2_recv, b2_send, b2_recv, q2_send, q2_recv,
-    local_sem, halo_sem, pair_sem, nz_sem, ny_sem, mz_sem, my_sem, mb_sem, z1_sem, y1_sem, yq_sem, y2_sem, z2_sem, zq_sem,
+    dw, a_sum, b_sum, c_sum, d_sum, fin, swap,
+    a1_send, a1_recv, b1_send, b1_recv, c1_send, c1_recv, d1_send, d1_recv,
+    a2_send, a2_recv, b2_send, b2_recv, c2_send, c2_recv, d2_send, d2_recv,
+    local_sem, halo_sem, pair_sem, nz_sem, ny_sem, mz_sem, my_sem, mb_sem, ring_z_sem, ring_y_sem, out_sem,
 ):
     ny, nz = lax.axis_size("y"), lax.axis_size("z")
     y, z, dp = lax.axis_index("y"), lax.axis_index("z"), lax.axis_index("dp")
@@ -249,13 +250,6 @@
     }
     score_scale = dim ** (-0.5)
 
-    barrier = pltpu.get_barrier_semaphore()
-    partners = [other, after, ahead_of]
-    partners += [{"z": lax.rem(z + j, nz)} for j in range(1, nz)]
-    partners += [{"y": lax.rem(y + j, ny)} for j in range(1, ny)]
-    for device in partners:
-        pl.semaphore_signal(barrier, inc=1, device_id=device, device_id_type=MESH)
-
     x_in = pltpu.make_async_copy(x_ref, x_all.at[pl.ds(0, tokens)], local_sem.at[0])
     cot_in = pltpu.make_async_copy(cot_ref, cot, local_sem.at[1])
     w_in = [
@@ -266,8 +260,13 @@
     for copy in w_in[:heads]:
         copy.start()
     cot_in.start()
-    for copy in w_in[heads:]:
-        copy.start()
+
+    barrier = pltpu.get_barrier_semaphore()
+    partners = [other, after, ahead_of]
+    partners += [{"z": lax.rem(z + j, nz)} for j in range(1, nz)]
+    partners += [{"y": lax.rem(y + j, ny)} for j in range(1, ny)]
+    for device in partners:
+        pl.semaphore_signal(barrier, inc=1, device_id=device, device_id_type=MESH)
 
     def project(at):
         for h in range(heads):
@@ -285,12 +284,12 @@
         )
 
     key_out = [halo_copy(kvq.at[h], prev.at[h], h, after) for h in range(heads)]
-    value_out = halo_copy(kvq.at[pl.ds(heads, heads)], prev.at[pl.ds(heads, heads)], heads, after)
+    value_out = [halo_copy(kvq.at[heads + h], prev.at[heads + h], heads + h, after) for h in range(heads)]
     local_out = [
-        halo_copy(grad_local.at[h], after_in.at[heads + h], heads + 1 + h, ahead_of) for h in range(heads)
+        halo_copy(grad_local.at[h], after_in.at[heads + h], 2 * heads + h, ahead_of) for h in range(heads)
     ]
-    query_out = halo_copy(kvq.at[pl.ds(2 * heads, heads)], after_in.at[pl.ds(0, heads)], 2 * heads + 1, ahead_of)
-    stats_out = halo_copy(stats, stats_in, 2 * heads + 2, ahead_of)
+    query_out = halo_copy(kvq.at[pl.ds(2 * heads, heads)], after_in.at[pl.ds(0, heads)], 3 * heads, ahead_of)
+    stats_out = [halo_copy(stats.at[h], stats_in.at[h], 3 * heads + 1 + h, ahead_of) for h in range(heads)]
 
     def pair_copy(src, dst, slot):
         return pltpu.make_async_remote_copy(
@@ -326,6 +325,8 @@
         return 1.0 / (1.0 + jnp.exp(-jnp.full((1, dim), gate_ref[h], jnp.float32)))
 
     x_in.wait()
+    for copy in w_in[heads:]:
+        copy.start()
     project(0)
 
     def key_sums(h):
@@ -381,18 +382,17 @@
         local_out[h].start()
     memory_scan.across_rows()
     memory_scan.give_back()
-    value_out.start()
+    for copy in value_out:
+        copy.start()
     query_out.start()
     grad_memory_scan.across_rows()
 
     x_out.wait_recv()
-    spans = 2 * tokens // dim
     tile = min(wide, 256)
 
     def turn(i, carry):
         at = pl.ds(pl.multiple_of(i * tile, 128), tile)
-        for c in range(spans):
-            w_all[c, at, :] = x_all[c * dim:(c + 1) * dim, at].T
+        x_turned[at, :] = x_all[:, at].T
         return carry
 
     lax.fori_loop(0, x_all.shape[1] // tile, turn, 0)
@@ -413,14 +413,10 @@
 
     each_head(retrieve)
     grad_norm_scan.start()
-    grad_memory_scan.give_back()
 
     segment, last = y * nz + z, ny * nz - 1
     bias = jnp.where(segment > 0, 0.0, MASKED)
     bias_after = jnp.where(segment < last, 0.0, MASKED)
-    for copy in key_out:
-        copy.wait_recv()
-    value_out.wait_recv()
 
     def as_row(column):
         return jnp.broadcast_to(column, (tokens, 128)).T[:1]
@@ -436,7 +432,7 @@
         p_own, p_prev = e_own * inverse, e_prev * inverse
         b_own, b_prev = p_own.astype(jnp.bfloat16), p_prev.astype(jnp.bfloat16)
         near = dot_nn(b_own, value) + dot_nn(b_prev, value_prev)
-        blended_ref[:, columns(h)] = (ret_mix[h] + (1.0 - mixing_of(h)) * near).astype(jnp.bfloat16)
+        blended[:, columns(h)] = (ret_mix[h] + (1.0 - mixing_of(h)) * near).astype(jnp.bfloat16)
         g_own, g_prev = soft_grads[h], dot_nt(local, value_prev)
         row_dot = jnp.sum(p_own * g_own, axis=1, keepdims=True) + jnp.sum(p_prev * g_prev, axis=1, keepdims=True)
         stats[h, 0:1] = as_row(top)
@@ -451,8 +447,15 @@
 
     for h in range(heads):
         stats[h] = jnp.zeros(stats.shape[1:], jnp.float32)
-    each_head(attend)
-    stats_out.start()
+    for h in range(heads):
+        key_out[h].wait_recv()
+        value_out[h].wait_recv()
+        attend(h)
+        stats_out[h].start()
+        if h == 0:
+            grad_memory_scan.give_back()
+    blended_out = pltpu.make_async_copy(blended, blended_ref, out_sem.at[6])
+    blended_out.start()
 
     def pair_grads(m):
         return pair_copy(grads.at[m, 1 - dp], g_all.at[m, pl.ds(tokens, tokens)], 1 + m)
@@ -461,49 +464,56 @@
         g_all[m, pl.ds(0, tokens), :] = grads[m, dp]
 
     def products(m, target):
-        def body(i, carry):
-            at = pl.multiple_of(target * wide + i * tile, 128)
-            total = dot_nn(w_all[0, pl.ds(at, tile), :], g_all[m, 0:dim, :])
-            for c in range(1, spans):
-                total = total + dot_nn(w_all[c, pl.ds(at, tile), :], g_all[m, c * dim:(c + 1) * dim, :])
-            dw[m, target, pl.ds(pl.multiple_of(i * tile, 8), tile), :] = total
-            return carry
-        lax.fori_loop(0, wide // tile, body, 0)
-
-    def a1_mine(target, sub):
-        return dw[1, :, pl.ds(pl.multiple_of(target * block + sub * rows, 8), rows), :]
-
-    def y_first(m):
-        return lambda target, sub: dw[m, target, sub * (wide // 2):(sub + 1) * (wide // 2), :]
+        at = pl.multiple_of(target * wide, 128)
+        dw[m, target] = dot_nn(x_turned[pl.ds(at, wide), :], g_all[m])
+
+    part = dim // 2
+
+    def z_first(m, left, right):
+        return lambda target, sub: dw[m, :, pl.ds(pl.multiple_of(target * block + sub * rows, 8), rows), left:right]
+
+    def y_first(m, left, right):
+        return lambda target, sub: dw[m, target, sub * (wide // 2):(sub + 1) * (wide // 2), left:right]
+
+    def y_second(held):
+        return lambda target, sub: held[sub, target]
 
     def z_second(held):
         return lambda target, sub: held[pl.ds(pl.multiple_of(target * block + sub * rows, 8), rows), :]
 
-    a1 = RingSum("z", a1_mine, a1_send, a1_recv, z1_sem.at[0], z1_sem.at[1])
-    b1 = RingSum("y", y_first(2), b1_send, b1_recv, y1_sem.at[0], y1_sem.at[1])
-    q1 = RingSum("y", y_first(0), q1_send, q1_recv, yq_sem.at[0], yq_sem.at[1])
-    a2 = RingSum("y", lambda k, sub: a_sum[sub, k], a2_send, a2_recv, y2_sem.at[0], y2_sem.at[1])
-    b2 = RingSum("z", z_second(b_sum), b2_send, b2_recv, z2_sem.at[0], z2_sem.at[1])
-    q2 = RingSum("z", z_second(q_sum), q2_send, q2_recv, zq_sem.at[0], zq_sem.at[1])
-
-    def rows_in(ring, held):
+    def ring(axis, slot, mine, send, recv):
+        sem = (ring_z_sem if axis == "z" else ring_y_sem).at[slot]
+        return RingSum(axis, mine, send, recv, sem.at[0], sem.at[1])
+
+    a1 = ring("z", 0, z_first(1, 0, dim), a1_send, a1_recv)
+    b1 = ring("y", 0, y_first(2, 0, dim), b1_send, b1_recv)
+    c1 = ring("z", 1, z_first(0, 0, part), c1_send, c1_recv)
+    d1 = ring("y", 1, y_first(0, part, dim), d1_send, d1_recv)
+    a2 = ring("y", 2, y_second(a_sum), a2_send, a2_recv)
+    b2 = ring("z", 2, z_second(b_sum), b2_send, b2_recv)
+    c2 = ring("y", 3, y_second(c_sum), c2_send, c2_recv)
+    d2 = ring("z", 3, z_second(d_sum), d2_send, d2_recv)
+
+    def columns_in(sums, held):
         for sub in (0, 1):
-            held[sub * (wide // 2):(sub + 1) * (wide // 2), :] = ring.total(sub)
+            held[sub] = sums.total(sub)
+
+    def multiply(m, first):
+        products(m, lax.rem(y + ny // 2, ny))
+        first.step(0, ny // 2)
+        for ahead in range(1, ny):
+            products(m, lax.rem(y + ny // 2 + ahead, ny))
+        for ahead in range(1, ny):
+            first.step(0, ny // 2 + ahead)
+
+    def rows_in(sums, held):
+        for sub in (0, 1):
+            held[sub * (wide // 2):(sub + 1) * (wide // 2), :] = sums.total(sub)
 
     query_pair = pair_grads(0)
     query_pair.start()
     keep_grads(0)
     grad_norm_scan.across_rows()
-    query_pair.wait_recv()
-    for step in range(ny):
-        ahead = ny // 2 - step
-        products(0, lax.rem(y + ahead + ny, ny))
-        q1.step(0, ahead)
-
-    for copy in local_out:
-        copy.wait_recv()
-    query_out.wait_recv()
-    stats_out.wait_recv()
 
     def serve(h):
         query, local = after_in[h], after_in[heads + h]
@@ -513,7 +523,15 @@
         own_grads[h] += dot_nn(given, query)
         own_grads[heads + h] += dot_nn(soft.astype(jnp.bfloat16), local)
 
-    each_head(serve)
+    query_out.wait_recv()
+    for h in range(heads):
+        if h == heads - 1:
+            query_pair.wait_recv()
+            multiply(0, d1)
+            c1.step(0)
+        local_out[h].wait_recv()
+        stats_out[h].wait_recv()
+        serve(h)
     norms[1] = grad_norm_scan.result()
     grad_memory_scan.finish()
 
@@ -525,56 +543,71 @@
         grad_value = dot_nn(feature(key).astype(jnp.bfloat16), grad_memory)
         grads[2, h] = (own_grads[heads + h] + grad_value).astype(jnp.bfloat16)
 
-    each_head(write_back)
+    write_back(1 - dp)
     key_pair, value_pair = pair_grads(1), pair_grads(2)
     key_pair.start()
     value_pair.start()
+    write_back(dp)
     keep_grads(1)
     keep_grads(2)
     key_pair.wait_recv()
     for k in range(ny):
         products(1, k)
+    c1.step(1)
     a1.step(0)
+    d1.step(1)
     value_pair.wait_recv()
-    for step in range(ny):
-        ahead = ny // 2 - step
-        products(2, lax.rem(y + ahead + ny, ny))
-        b1.step(0, ahead)
-    q1.step(1)
+    multiply(2, b1)
+    c1.step(2)
+    rows_in(d1, d_sum)
+    d2.step(0)
     a1.step(1)
-    rows_in(q1, q_sum)
-    q2.step(0)
+    c1.step(3)
+    b1.step(1)
+    d2.step(1)
     a1.step(2)
-    b1.step(1)
-    q2.step(1)
+    columns_in(c1, c_sum)
+    c2.step(0)
+    d2.step(2)
     a1.step(3)
-    q2.step(2)
+    d2.step(3)
     rows_in(b1, b_sum)
     b2.step(0)
-    for sub in (0, 1):
-        a_sum[sub] = a1.total(sub)
+    c2.step(1)
+    columns_in(a1, a_sum)
     a2.step(0)
-    q2.step(3)
     b2.step(1)
     a2.step(1)
     for t in range(2, nz // 2):
         b2.step(t)
-    for sub in (0, 1):
-        for m, ring in enumerate((q2, a2, b2)):
-            fin[sub, :, m * dim:(m + 1) * dim] = ring.total(sub) * scale
+    places = ((c2, 0, part), (d2, part, dim), (a2, dim, 2 * dim), (b2, 2 * dim, 3 * dim))
+    for sums, left, right in places:
+        for sub in (0, 1):
+            fin[sub, :, left:right] = sums.total(sub) * scale
     swap_out = pair_copy(fin.at[1 - dp], swap, 4)
     swap_out.start()
-    for m in range(3):
-        out_ref[m, :, columns(dp)] = fin[dp, :, m * dim:(m + 1) * dim]
+
+    def put(src, m, place, slot):
+        return pltpu.make_async_copy(
+            src.at[:, pl.ds(m * dim, dim)], out_ref.at[m, :, columns(place)], out_sem.at[slot]
+        )
+
+    own_out = [put(fin.at[dp], m, dp, m) for m in range(3)]
+    other_out = [put(swap, m, 1 - dp, 3 + m) for m in range(3)]
+    for copy in own_out:
+        copy.start()
     for sent in (
-        a1, b1, q1, a2, b2, q2, norm_scan, grad_norm_scan, memory_scan, grad_memory_scan,
+        a1, b1, c1, d1, a2, b2, c2, d2, norm_scan, grad_norm_scan, memory_scan, grad_memory_scan,
     ):
         sent.drain()
-    for copy in (*key_out, value_out, *local_out, query_out, stats_out, x_out, query_pair, key_pair, value_pair):
+    for copy in (*key_out, *value_out, *local_out, query_out, *stats_out, x_out, query_pair, key_pair, value_pair):
         copy.wait_send()
-    swap_out.wait()
-    for m in range(3):
-        out_ref[m, :, columns(1 - dp)] = swap[:, m * dim:(m + 1) * dim]
+    swap_out.wait_recv()
+    for copy in other_out:
+        copy.start()
+    swap_out.wait_send()
+    for copy in (*own_out, *other_out, blended_out):
+        copy.wait()
 
 
 def layer(x, wq, wk, wv, gate, cot, scale):
@@ -588,7 +621,7 @@
     wire = lambda *shape: pltpu.VMEM(shape, jnp.bfloat16)
     real = lambda *shape: pltpu.VMEM(shape, jnp.float32)
     dma = lambda *shape: pltpu.SemaphoreType.DMA(shape)
-    a1, b1, last = (zs, ny, rows, dim), (ys, wide // 2, dim), (rows, dim)
+    a1, b1 = (zs, ny, rows), (ys, wide // 2)
     part = (heads * dim // nz, dim)
     vectors = [real(heads, 1, dim), real(nz, heads, 1, dim), real(heads, 1, dim), real(ny, heads, 1, dim)]
     scan = [
@@ -604,22 +637,24 @@
             jax.ShapeDtypeStruct((3, rows, heads * dim), jnp.float32),
         ),
         in_specs=[anywhere] * 4 + [pl.BlockSpec(memory_space=pltpu.SMEM), anywhere],
-        out_specs=(pl.BlockSpec(memory_space=pltpu.VMEM),) * 2,
+        out_specs=(anywhere,) * 2,
         scratch_shapes=[
-            wire(2 * tokens, depth), wire(3 * heads, depth, dim), wire(tokens, heads * dim),
+            wire(2 * tokens, depth), wire(depth, 2 * tokens), wire(3 * heads, depth, dim), wire(tokens, heads * dim), wire(tokens, heads * dim),
             wire(3 * heads, tokens, dim), wire(*pair), wire(*pair), real(*pair),
             real(heads, tokens, dim), real(heads, tokens, dim),
             real(heads, tokens, tokens), real(heads, tokens, tokens), wire(heads, tokens, dim),
             wire(heads, tokens, dim), real(heads, tokens, 1), real(heads, 8, tokens), real(heads, 8, tokens),
             wire(3, heads, tokens, dim), wire(3, 2 * tokens, dim),
             *vectors, *vectors, real(2, heads, 1, dim), *scan, *scan,
-            real(3, ny, wide, dim), real(2, ny, rows, dim), real(wide, dim), real(wide, dim),
+            real(3, ny, wide, dim), real(2, ny, rows, dim), real(wide, dim), real(2, ny, rows, dim // 2), real(wide, dim // 2),
             real(2, rows, 3 * dim), real(rows, 3 * dim),
-            wire(*a1), wire(*a1), wire(*b1), wire(*b1), wire(*b1), wire(*b1),
-            wire(ys, *last), wire(ys, *last), wire(zs, *last), wire(zs, *last), wire(zs, *last), wire(zs, *last),
-            dma(2 + 3 * heads), dma(2, 2 * heads + 3), dma(2, 5), dma(2, 2, nz), dma(2, 2, ny),
+            wire(*a1, dim), wire(*a1, dim), wire(*b1, dim), wire(*b1, dim),
+            wire(*a1, dim // 2), wire(*a1, dim // 2), wire(*b1, dim // 2), wire(*b1, dim // 2),
+            wire(ys, rows, dim), wire(ys, rows, dim), wire(zs, rows, dim), wire(zs, rows, dim),
+            wire(ys, rows, dim // 2), wire(ys, rows, dim // 2), wire(zs, rows, dim // 2), wire(zs, rows, dim // 2),
+            dma(2 + 3 * heads), dma(2, 4 * heads + 1), dma(2, 5), dma(2, 2, nz), dma(2, 2, ny),
             dma(2, 2, nz), dma(2, 2, ny), dma(2, 2, nz),
-            dma(2, zs), dma(2, ys), dma(2, ys), dma(2, ys), dma(2, zs), dma(2, zs),
+            dma(4, 2, zs), dma(4, 2, ys), dma(7),
         ],
         compiler_params=pltpu.CompilerParams(
             collective_id=1, has_side_effects=True, vmem_limit_bytes=63 * 1024 * 1024
@@ -627,11 +662,37 @@
     )(x, wq, wk, wv, gate, cot)
 
 
+def hand_on_kernel(a_ref, b_ref, a_out, b_out, a_held, b_held, sem):
+    steps = [
+        (pltpu.make_async_copy(src, held, sem.at[0, i]), pltpu.make_async_copy(held, dst, sem.at[1, i]))
+        for i, (src, held, dst) in enumerate(((a_ref, a_held, a_out), (b_ref, b_held, b_out)))
+    ]
+    for first, _ in steps:
+        first.start()
+    for first, second in steps:
+        first.wait()
+        second.start()
+    for _, second in steps:
+        second.wait()
+
+
+def hand_on(a, b):
+    anywhere = pl.BlockSpec(memory_space=pl.ANY)
+    return pl.pallas_call(
+        hand_on_kernel,
+        out_shape=tuple(jax.ShapeDtypeStruct(v.shape, v.dtype) for v in (a, b)),
+        in_specs=[anywhere] * 2,
+        out_specs=(anywhere,) * 2,
+        scratch_shapes=[pltpu.VMEM(v.shape, v.dtype) for v in (a, b)] + [pltpu.SemaphoreType.DMA((2, 2))],
+    )(a, b)
+
+
 def local(inputs, w_query, w_key, w_value, gate_bias, cotangent):
     tokens = inputs[0]
     seg_len = tokens.shape[0]
     scale = 1.0 / math.sqrt(lax.axis_size(SEQ) * lax.axis_size("dp") * seg_len)
     blended, grad_weights = layer(tokens, w_query, w_key, w_value, gate_bias, cotangent[0], scale)
+    blended, grad_weights = hand_on(blended, grad_weights)
     return (blended[None], grad_weights.transpose(1, 0, 2))
 
 

time: 111 us -> 102 us (0.919)
  Pallas kernels: 107 us -> 101 us
  local copies, waits for them, and re-layouts: 3.46 us -> 0 us
    pallas_call x1, Pallas kernels: 107 us -> 99.4 us  [layer(): pl.pallas_call(functools.partial(layer_kernel, scale), out_shape=(jax.Sha...]
    unnamed x2 -> x0, local copies, waits for them, and re-layouts: 3.46 us -> none
    pallas_call x0 -> x1, Pallas kernels: none -> 1.87 us  [hand_on(): pl.pallas_call(hand_on_kernel, out_shape=tuple((jax.ShapeDtypeStruct(v.sh...]
where the time goes in v4:
time: 102 us
  Pallas kernels  101 us (99%)
    pallas_call x1, Pallas kernels, layer(): pl.pallas_call(functools.partial(layer_kernel, scale), out_shape=(jax.Sha...  99.4 us

profile of v4, /device:TPU:1, one launch (start us, length us, event | category | flops | bytes accessed | tf_op | source)
XLA Modules:
  0.0 102.1 jit_solution(7357821779908388081)
XLA Ops:
  0.6 99.4 %shard_map.77 = (bf16[384,512]{1,0:T(8,128)(2,1)}, f32[3,48,512]{2,1,0:T(8,128)}) custom-call(bf16[384,3072]{1,0:T(8,128)(2,1)} %bitcast.4, bf16[3072,512]{1,0:T(8,128)(2,1)} %wq_ref.1, bf16[3072,512]{1,0:T(8,128)(2,1)} %wk_ref.1, bf16[3072,512]{1,0:T(8,128)(2,1)} %wv_ref.1, f32[2]{0:T(128)} %gate_ref.1, bf16[384,512]{1,0:T(8,128)(2,1)} %bitcast.5), custom_call_target="tpu_custom_call" | custom-call | tf_op jit(solution)/shard_map/pallas_call | solution.py:633
  100.0 1.9 %shard_map.78 = (bf16[384,512]{1,0:T(8,128)(2,1)}, f32[3,48,512]{2,1,0:T(8,128)}) custom-call(bf16[384,512]{1,0:T(8,128)(2,1)} %get-tuple-element.6.a_ref, f32[3,48,512]{2,1,0:T(8,128)} %get-tuple-element.7.b_ref), custom_call_target="tpu_custom_call" | custom-call | tf_op jit(solution)/shard_map/pallas_call | solution.py:681

commit v5 on v4

--- a/solution.py
+++ b/solution.py
@@ -62,7 +62,7 @@
         return pltpu.make_async_remote_copy(
             src_ref=self.send.at[slot],
             dst_ref=self.recv.at[slot],
-            send_sem=self.send_sem.at[slot],
+            send_sem=self.send_sem,
             recv_sem=self.recv_sem.at[slot],
             device_id={self.axis: lax.rem(self.position + way + self.n, self.n)},
             device_id_type=MESH,
@@ -91,9 +91,13 @@
         return value
 
     def drain(self):
-        for _, way, length, first in self.chains:
-            for t in range(length):
-                self.copy(first + t, way).wait_send()
+        self.all_copy().wait_send()
+
+    def all_copy(self):
+        return pltpu.make_async_remote_copy(
+            src_ref=self.send, dst_ref=self.recv, send_sem=self.send_sem, recv_sem=self.recv_sem.at[0],
+            device_id={self.axis: self.position}, device_id_type=MESH,
+        )
 
 
 class Spread:
@@ -105,21 +109,27 @@
         return pltpu.make_async_remote_copy(
             src_ref=src,
             dst_ref=self.got.at[j],
-            send_sem=self.sem.at[0, j],
-            recv_sem=self.sem.at[1, j],
+            send_sem=self.sem.at[0],
+            recv_sem=self.sem.at[1],
             device_id={self.axis: lax.rem(self.position + j, self.n)},
             device_id_type=MESH,
         )
 
+    def all_copy(self):
+        others = self.got.at[pl.ds(1, self.n - 1)]
+        return pltpu.make_async_remote_copy(
+            src_ref=others, dst_ref=others, send_sem=self.sem.at[0], recv_sem=self.sem.at[1],
+            device_id={self.axis: self.position}, device_id_type=MESH,
+        )
+
     def start(self, src):
-        self.src = src
         for j in range(1, self.n):
             self.copy(src, j).start()
 
     def sums(self, own, reverse):
         passed, total = jnp.zeros_like(own), own
+        self.all_copy().wait_recv()
         for j in range(1, self.n):
-            self.copy(self.src, j).wait_recv()
             value = self.got[j]
             earlier = self.position < j if reverse else self.position >= j
             passed = passed + value * jnp.where(earlier, 1.0, 0.0)
@@ -127,8 +137,7 @@
         return passed, total
 
     def drain(self):
-        for j in range(1, self.n):
-            self.copy(self.src, j).wait_send()
+        self.all_copy().wait_send()
 
 
 class VectorScan:
@@ -165,8 +174,8 @@
         return pltpu.make_async_remote_copy(
             src_ref=self.parts.at[target],
             dst_ref=self.got.at[j],
-            send_sem=self.z_sem.at[0, j],
-            recv_sem=self.z_sem.at[1, j],
+            send_sem=self.z_sem.at[0],
+            recv_sem=self.z_sem.at[1],
             device_id={"z": target},
             device_id_type=MESH,
         )
@@ -176,8 +185,8 @@
         return pltpu.make_async_remote_copy(
             src_ref=self.back.at[target],
             dst_ref=self.full.at[self.position],
-            send_sem=self.back_sem.at[0, j],
-            recv_sem=self.back_sem.at[1, j],
+            send_sem=self.back_sem.at[0],
+            recv_sem=self.back_sem.at[1],
             device_id={"z": target},
             device_id_type=MESH,
         )
@@ -187,8 +196,7 @@
             self.out_copy(j).start()
 
     def across_rows(self):
-        for j in range(1, self.n):
-            self.out_copy(j).wait_recv()
+        self.all_copy(self.z_sem).wait_recv()
         self.got[0] = self.parts[self.position]
         run = jnp.zeros(self.y_own.shape, jnp.float32)
         for k in reversed(range(self.n)) if self.reverse else range(self.n):
@@ -206,8 +214,7 @@
         self.full[self.position] = self.back[self.position]
 
     def finish(self):
-        for j in range(1, self.n):
-            self.back_copy(j).wait_recv()
+        self.all_copy(self.back_sem).wait_recv()
 
     def head(self, h, heads):
         parts = self.n // heads
@@ -216,9 +223,15 @@
 
     def drain(self):
         self.y.drain()
-        for j in range(1, self.n):
-            self.out_copy(j).wait_send()
-            self.back_copy(j).wait_send()
+        self.all_copy(self.z_sem).wait_send()
+        self.all_copy(self.back_sem).wait_send()
+
+    def all_copy(self, sem):
+        others = self.got.at[pl.ds(1, self.n - 1)]
+        return pltpu.make_async_remote_copy(
+            src_ref=others, dst_ref=others, send_sem=sem.at[0], recv_sem=sem.at[1],
+            device_id={"z": self.position}, device_id_type=MESH,
+        )
 
 
 def layer_kernel(
@@ -231,7 +244,7 @@
     dw, a_sum, b_sum, c_sum, d_sum, fin, swap,
     a1_send, a1_recv, b1_send, b1_recv, c1_send, c1_recv, d1_send, d1_recv,
     a2_send, a2_recv, b2_send, b2_recv, c2_send, c2_recv, d2_send, d2_recv,
-    local_sem, halo_sem, pair_sem, nz_sem, ny_sem, mz_sem, my_sem, mb_sem, ring_z_sem, ring_y_sem, out_sem,
+    local_sem, halo_sem, pair_sem, nz_sem, ny_sem, mz_sem, my_sem, mb_sem, ring_z_sem, ring_y_sem, ring_send_sem, out_sem,
 ):
     ny, nz = lax.axis_size("y"), lax.axis_size("z")
     y, z, dp = lax.axis_index("y"), lax.axis_index("z"), lax.axis_index("dp")
@@ -257,8 +270,7 @@
         for at, w in enumerate((wk_ref, wv_ref, wq_ref)) for h in range(heads)
     ]
     x_in.start()
-    for copy in w_in[:heads]:
-        copy.start()
+    w_in[0].start()
     cot_in.start()
 
     barrier = pltpu.get_barrier_semaphore()
@@ -268,14 +280,13 @@
     for device in partners:
         pl.semaphore_signal(barrier, inc=1, device_id=device, device_id_type=MESH)
 
-    def project(at):
-        for h in range(heads):
-            w_in[at * heads + h].wait()
-        def body(h, carry):
-            c = at * heads + h
+    def project(first, last):
+        for c in range(first, last):
+            w_in[c].wait()
+        def body(c, carry):
             kvq[c] = dot_nn(x_all[pl.ds(0, tokens), :], w_all[c]).astype(jnp.bfloat16)
             return carry
-        lax.fori_loop(0, heads, body, 0)
+        lax.fori_loop(first, last, body, 0)
 
     def halo_copy(src, dst, slot, device):
         return pltpu.make_async_remote_copy(
@@ -325,14 +336,8 @@
         return 1.0 / (1.0 + jnp.exp(-jnp.full((1, dim), gate_ref[h], jnp.float32)))
 
     x_in.wait()
-    for copy in w_in[heads:]:
+    for copy in w_in[1:]:
         copy.start()
-    project(0)
-
-    def key_sums(h):
-        n1_own[h] = jnp.sum(feature(kvq[h].astype(jnp.float32)), axis=0, keepdims=True)
-
-    each_head(key_sums)
     cot_in.wait()
 
     def local_gradient(h):
@@ -340,13 +345,20 @@
         grad_local[h] = ((1.0 - mixing_of(h)) * upstream).astype(jnp.bfloat16)
 
     each_head(local_gradient)
+    project(0, 1)
     pl.semaphore_wait(barrier, len(partners))
-    norm_scan.start()
     key_out[0].start()
     local_out[0].start()
+    project(1, heads)
+
+    def key_sums(h):
+        n1_own[h] = jnp.sum(feature(kvq[h].astype(jnp.float32)), axis=0, keepdims=True)
+
+    each_head(key_sums)
+    norm_scan.start()
     x_out = pair_copy(x_all.at[pl.ds(0, tokens)], x_all.at[pl.ds(tokens, tokens)], 0)
     x_out.start()
-    project(1)
+    project(heads, 2 * heads)
 
     def write(h):
         phi = feature(kvq[h].astype(jnp.float32)).astype(jnp.bfloat16)
@@ -354,7 +366,10 @@
 
     each_head(write)
     memory_scan.start()
-    project(2)
+    for h in range(1, heads):
+        key_out[h].start()
+        local_out[h].start()
+    project(2 * heads, 3 * heads)
     norm_scan.across_rows()
 
     def own_part(h):
@@ -377,15 +392,11 @@
 
     each_head(memory_gradient)
     grad_memory_scan.start()
-    for h in range(1, heads):
-        key_out[h].start()
-        local_out[h].start()
     memory_scan.across_rows()
     memory_scan.give_back()
     for copy in value_out:
         copy.start()
     query_out.start()
-    grad_memory_scan.across_rows()
 
     x_out.wait_recv()
     tile = min(wide, 256)
@@ -396,6 +407,7 @@
         return carry
 
     lax.fori_loop(0, x_all.shape[1] // tile, turn, 0)
+    grad_memory_scan.across_rows()
     memory_scan.finish()
 
     def retrieve(h):
@@ -454,7 +466,7 @@
         stats_out[h].start()
         if h == 0:
             grad_memory_scan.give_back()
-    blended_out = pltpu.make_async_copy(blended, blended_ref, out_sem.at[6])
+    blended_out = pltpu.make_async_copy(blended, blended_ref, out_sem.at[2])
     blended_out.start()
 
     def pair_grads(m):
@@ -483,7 +495,8 @@
 
     def ring(axis, slot, mine, send, recv):
         sem = (ring_z_sem if axis == "z" else ring_y_sem).at[slot]
-        return RingSum(axis, mine, send, recv, sem.at[0], sem.at[1])
+        at = slot if axis == "z" else 4 + slot
+        return RingSum(axis, mine, send, recv, ring_send_sem.at[at], sem)
 
     a1 = ring("z", 0, z_first(1, 0, dim), a1_send, a1_recv)
     b1 = ring("y", 0, y_first(2, 0, dim), b1_send, b1_recv)
@@ -562,24 +575,24 @@
     rows_in(d1, d_sum)
     d2.step(0)
     a1.step(1)
+    b1.step(1)
     c1.step(3)
-    b1.step(1)
     d2.step(1)
     a1.step(2)
     columns_in(c1, c_sum)
     c2.step(0)
     d2.step(2)
+    rows_in(b1, b_sum)
+    b2.step(0)
     a1.step(3)
     d2.step(3)
-    rows_in(b1, b_sum)
-    b2.step(0)
+    b2.step(1)
     c2.step(1)
     columns_in(a1, a_sum)
     a2.step(0)
-    b2.step(1)
+    b2.step(2)
     a2.step(1)
-    for t in range(2, nz // 2):
-        b2.step(t)
+    b2.step(3)
     places = ((c2, 0, part), (d2, part, dim), (a2, dim, 2 * dim), (b2, 2 * dim, 3 * dim))
     for sums, left, right in places:
         for sub in (0, 1):
@@ -592,8 +605,8 @@
             src.at[:, pl.ds(m * dim, dim)], out_ref.at[m, :, columns(place)], out_sem.at[slot]
         )
 
-    own_out = [put(fin.at[dp], m, dp, m) for m in range(3)]
-    other_out = [put(swap, m, 1 - dp, 3 + m) for m in range(3)]
+    own_out = [put(fin.at[dp], m, dp, 0) for m in range(3)]
+    other_out = [put(swap, m, 1 - dp, 1) for m in range(3)]
     for copy in own_out:
         copy.start()
     for sent in (
@@ -606,8 +619,9 @@
     for copy in other_out:
         copy.start()
     swap_out.wait_send()
-    for copy in (*own_out, *other_out, blended_out):
-        copy.wait()
+    blended_out.wait()
+    for slot in (0, 1):
+        pltpu.make_async_copy(fin.at[slot], swap, out_sem.at[slot]).wait()
 
 
 def layer(x, wq, wk, wv, gate, cot, scale):
@@ -652,9 +666,9 @@
             wire(*a1, dim // 2), wire(*a1, dim // 2), wire(*b1, dim // 2), wire(*b1, dim // 2),
             wire(ys, rows, dim), wire(ys, rows, dim), wire(zs, rows, dim), wire(zs, rows, dim),
             wire(ys, rows, dim // 2), wire(ys, rows, dim // 2), wire(zs, rows, dim // 2), wire(zs, rows, dim // 2),
-            dma(2 + 3 * heads), dma(2, 4 * heads + 1), dma(2, 5), dma(2, 2, nz), dma(2, 2, ny),
-            dma(2, 2, nz), dma(2, 2, ny), dma(2, 2, nz),
-            dma(4, 2, zs), dma(4, 2, ys), dma(7),
+            dma(2 + 3 * heads), dma(2, 4 * heads + 1), dma(2, 5), dma(2, 2), dma(2, 2),
+            dma(2, 2), dma(2, 2), dma(2, 2),
+            dma(4, zs), dma(4, ys), dma(8), dma(3),
         ],
         compiler_params=pltpu.CompilerParams(
             collective_id=1, has_side_effects=True, vmem_limit_bytes=63 * 1024 * 1024

time: 102 us -> 96.5 us (0.946)
  Pallas kernels: 101 us -> 95.6 us
    pallas_call x1, Pallas kernels: 99.4 us -> 93.7 us  [layer(): pl.pallas_call(functools.partial(layer_kernel, scale), out_shape=(jax.Sha...]
where the time goes in v5:
time: 96.5 us; the launch traced here: 96.4 us
  Pallas kernels  95.6 us (99%)
    pallas_call x1, Pallas kernels, layer(): pl.pallas_call(functools.partial(layer_kernel, scale), out_shape=(jax.Sha...  93.7 us

profile of v5, /device:TPU:1, one launch (start us, length us, event | category | flops | bytes accessed | tf_op | source)
XLA Modules:
  0.0 96.4 jit_solution(5837901437476919916)
XLA Ops:
  0.6 93.7 %shard_map.77 = (bf16[384,512]{1,0:T(8,128)(2,1)}, f32[3,48,512]{2,1,0:T(8,128)}) custom-call(bf16[384,3072]{1,0:T(8,128)(2,1)} %bitcast.4, bf16[3072,512]{1,0:T(8,128)(2,1)} %wq_ref.1, bf16[3072,512]{1,0:T(8,128)(2,1)} %wk_ref.1, bf16[3072,512]{1,0:T(8,128)(2,1)} %wv_ref.1, f32[2]{0:T(128)} %gate_ref.1, bf16[384,512]{1,0:T(8,128)(2,1)} %bitcast.5), custom_call_target="tpu_custom_call" | custom-call | tf_op jit(solution)/shard_map/pallas_call | solution.py:647
  94.4 1.9 %shard_map.78 = (bf16[384,512]{1,0:T(8,128)(2,1)}, f32[3,48,512]{2,1,0:T(8,128)}) custom-call(bf16[384,512]{1,0:T(8,128)(2,1)} %get-tuple-element.6.a_ref, f32[3,48,512]{2,1,0:T(8,128)} %get-tuple-element.7.b_ref), custom_call_target="tpu_custom_call" | custom-call | tf_op jit(solution)/shard_map/pallas_call | solution.py:695

commit v6 on v5

--- a/solution.py
+++ b/solution.py
@@ -13,6 +13,7 @@
 SEQ_DP = ("y", "z", "dp")
 MESH = pl.DeviceIdType.MESH
 MASKED = -1e30
+PIECES = 4
 
 
 def feature(u):
@@ -162,6 +163,29 @@
         self.y.drain()
 
 
+class VectorScanDown:
+    def __init__(self, reverse, own, y_got, z_own, z_got, y_sem, z_sem):
+        self.reverse, self.own, self.z_own = reverse, own, z_own
+        self.y, self.z = Spread("y", y_got, y_sem), Spread("z", z_got, z_sem)
+
+    def start(self):
+        self.y.start(self.own)
+
+    def across_columns(self):
+        passed, _ = self.y.sums(self.own[...], self.reverse)
+        self.z_own[0] = self.own[...]
+        self.z_own[1] = passed
+        self.z.start(self.z_own)
+
+    def result(self):
+        passed, total = self.z.sums(self.z_own[...], self.reverse)
+        return passed[0] + total[1]
+
+    def drain(self):
+        self.y.drain()
+        self.z.drain()
+
+
 class MemoryScan:
     def __init__(self, reverse, parts, got, inside, y_own, y_got, back, result, z_sem, y_sem, back_sem):
         self.reverse, self.parts, self.got, self.inside, self.y_own = reverse, parts, got, inside, y_own
@@ -236,15 +260,15 @@
 
 def layer_kernel(
     scale, x_ref, wq_ref, wk_ref, wv_ref, gate_ref, cot_ref, blended_ref, out_ref,
-    x_all, x_turned, w_all, cot, blended, kvq, prev, after_in, own_grads, dq_ret, ret_mix,
+    x_all, x_turned, w_all, cot, blended, kvq, prev, after_in, own_grads, dq_att, near_mix,
     scores, soft_grads, grad_local, grad_num, den, stats, stats_in, grads, g_all,
-    n1_own, n1_got, n1_yown, n1_ygot, n2_own, n2_got, n2_yown, n2_ygot, norms,
+    n1_own, n1_got, n1_yown, n1_ygot, n2_own, n2_ygot, n2_zown, n2_zgot, norms,
     m1_parts, m1_got, m1_inside, m1_yown, m1_ygot, m1_back, m1_full,
     m2_parts, m2_got, m2_inside, m2_yown, m2_ygot, m2_back, m2_full,
     dw, a_sum, b_sum, c_sum, d_sum, fin, swap,
     a1_send, a1_recv, b1_send, b1_recv, c1_send, c1_recv, d1_send, d1_recv,
     a2_send, a2_recv, b2_send, b2_recv, c2_send, c2_recv, d2_send, d2_recv,
-    local_sem, halo_sem, pair_sem, nz_sem, ny_sem, mz_sem, my_sem, mb_sem, ring_z_sem, ring_y_sem, ring_send_sem, out_sem,
+    local_sem, halo_sem, pair_sem, nz_sem, ny_sem, mz_sem, my_sem, mb_sem, ring_z_sem, ring_y_sem, ring_send_sem, direct_sem, out_sem,
 ):
     ny, nz = lax.axis_size("y"), lax.axis_size("z")
     y, z, dp = lax.axis_index("y"), lax.axis_index("z"), lax.axis_index("dp")
@@ -299,8 +323,8 @@
     local_out = [
         halo_copy(grad_local.at[h], after_in.at[heads + h], 2 * heads + h, ahead_of) for h in range(heads)
     ]
-    query_out = halo_copy(kvq.at[pl.ds(2 * heads, heads)], after_in.at[pl.ds(0, heads)], 3 * heads, ahead_of)
-    stats_out = [halo_copy(stats.at[h], stats_in.at[h], 3 * heads + 1 + h, ahead_of) for h in range(heads)]
+    query_out = [halo_copy(kvq.at[2 * heads + h], after_in.at[h], 3 * heads + h, ahead_of) for h in range(heads)]
+    stats_out = [halo_copy(stats.at[h], stats_in.at[h], 4 * heads + h, ahead_of) for h in range(heads)]
 
     def pair_copy(src, dst, slot):
         return pltpu.make_async_remote_copy(
@@ -318,7 +342,7 @@
         return pl.ds(pl.multiple_of(h * dim, dim), dim)
 
     norm_scan = VectorScan(False, n1_own, n1_got, n1_yown, n1_ygot, nz_sem.at[0], ny_sem.at[0])
-    grad_norm_scan = VectorScan(True, n2_own, n2_got, n2_yown, n2_ygot, nz_sem.at[1], ny_sem.at[1])
+    grad_norm_scan = VectorScanDown(True, n2_own, n2_ygot, n2_zown, n2_zgot, ny_sem.at[1], nz_sem.at[1])
     memory_scan = MemoryScan(
         False, m1_parts, m1_got, m1_inside, m1_yown, m1_ygot, m1_back, m1_full,
         mz_sem.at[0], my_sem.at[0], mb_sem.at[0],
@@ -392,11 +416,13 @@
 
     each_head(memory_gradient)
     grad_memory_scan.start()
+    value_out[0].start()
+    query_out[0].start()
     memory_scan.across_rows()
     memory_scan.give_back()
-    for copy in value_out:
-        copy.start()
-    query_out.start()
+    for h in range(1, heads):
+        value_out[h].start()
+        query_out[h].start()
 
     x_out.wait_recv()
     tile = min(wide, 256)
@@ -408,23 +434,6 @@
 
     lax.fori_loop(0, x_all.shape[1] // tile, turn, 0)
     grad_memory_scan.across_rows()
-    memory_scan.finish()
-
-    def retrieve(h):
-        mixing = mixing_of(h)
-        query = kvq[2 * heads + h].astype(jnp.float32)
-        phi = feature(query)
-        memory = memory_scan.head(h, heads)
-        retrieved = dot_nn(phi.astype(jnp.bfloat16), memory) / den[h]
-        ret_mix[h] = mixing * retrieved
-        grad_ret = mixing * cot[:, columns(h)].astype(jnp.float32)
-        grad_den = -jnp.sum(grad_ret * retrieved, axis=1, keepdims=True) / den[h]
-        n2_own[h] = jnp.sum(grad_den * phi, axis=0, keepdims=True)
-        grad_phi = dot_nt(grad_num[h], memory) + grad_den * norms[0, h]
-        dq_ret[h] = grad_phi * feature_slope(query)
-
-    each_head(retrieve)
-    grad_norm_scan.start()
 
     segment, last = y * nz + z, ny * nz - 1
     bias = jnp.where(segment > 0, 0.0, MASKED)
@@ -432,6 +441,21 @@
 
     def as_row(column):
         return jnp.broadcast_to(column, (tokens, 128)).T[:1]
+
+    seen = set()
+
+    def join(h, output, grad):
+        kind = (h, output is None)
+        if kind not in seen:
+            seen.add(kind)
+            if output is None:
+                dq_att[h] = grad
+            else:
+                near_mix[h] = output
+        elif output is None:
+            grads[0, h] = (dq_att[h] + grad).astype(jnp.bfloat16)
+        else:
+            blended[:, columns(h)] = (near_mix[h] + output).astype(jnp.bfloat16)
 
     def attend(h):
         query, key, value = kvq[2 * heads + h], kvq[h], kvq[heads + h]
@@ -444,7 +468,7 @@
         p_own, p_prev = e_own * inverse, e_prev * inverse
         b_own, b_prev = p_own.astype(jnp.bfloat16), p_prev.astype(jnp.bfloat16)
         near = dot_nn(b_own, value) + dot_nn(b_prev, value_prev)
-        blended[:, columns(h)] = (ret_mix[h] + (1.0 - mixing_of(h)) * near).astype(jnp.bfloat16)
+        join(h, (1.0 - mixing_of(h)) * near, None)
         g_own, g_prev = soft_grads[h], dot_nt(local, value_prev)
         row_dot = jnp.sum(p_own * g_own, axis=1, keepdims=True) + jnp.sum(p_prev * g_prev, axis=1, keepdims=True)
         stats[h, 0:1] = as_row(top)
@@ -454,21 +478,10 @@
         d_prev = (p_prev * (g_prev - row_dot) * score_scale).astype(jnp.bfloat16)
         own_grads[h] = dot_tn(d_own, query)
         own_grads[heads + h] = dot_tn(b_own, local)
-        dq_att = dot_nn(d_own, key) + dot_nn(d_prev, key_prev)
-        grads[0, h] = (dq_att + dq_ret[h]).astype(jnp.bfloat16)
+        join(h, None, dot_nn(d_own, key) + dot_nn(d_prev, key_prev))
 
     for h in range(heads):
         stats[h] = jnp.zeros(stats.shape[1:], jnp.float32)
-    for h in range(heads):
-        key_out[h].wait_recv()
-        value_out[h].wait_recv()
-        attend(h)
-        stats_out[h].start()
-        if h == 0:
-            grad_memory_scan.give_back()
-    blended_out = pltpu.make_async_copy(blended, blended_ref, out_sem.at[2])
-    blended_out.start()
-
     def pair_grads(m):
         return pair_copy(grads.at[m, 1 - dp], g_all.at[m, pl.ds(tokens, tokens)], 1 + m)
 
@@ -486,9 +499,6 @@
 
     def y_first(m, left, right):
         return lambda target, sub: dw[m, target, sub * (wide // 2):(sub + 1) * (wide // 2), left:right]
-
-    def y_second(held):
-        return lambda target, sub: held[sub, target]
 
     def z_second(held):
         return lambda target, sub: held[pl.ds(pl.multiple_of(target * block + sub * rows, 8), rows), :]
@@ -502,18 +512,32 @@
     b1 = ring("y", 0, y_first(2, 0, dim), b1_send, b1_recv)
     c1 = ring("z", 1, z_first(0, 0, part), c1_send, c1_recv)
     d1 = ring("y", 1, y_first(0, part, dim), d1_send, d1_recv)
-    a2 = ring("y", 2, y_second(a_sum), a2_send, a2_recv)
+    a2 = Spread("y", a2_recv, direct_sem.at[0])
     b2 = ring("z", 2, z_second(b_sum), b2_send, b2_recv)
-    c2 = ring("y", 3, y_second(c_sum), c2_send, c2_recv)
+    c2 = Spread("y", c2_recv, direct_sem.at[1])
     d2 = ring("z", 3, z_second(d_sum), d2_send, d2_recv)
 
     def columns_in(sums, held):
         for sub in (0, 1):
             held[sub] = sums.total(sub)
 
-    def multiply(m, first):
+    def send_parts(spread, held, parts):
+        for j in range(1, ny):
+            parts[j] = held[:, lax.rem(y + j, ny)].astype(jnp.bfloat16)
+            spread.copy(parts.at[j], j).start()
+
+    def direct_total(spread, held):
+        spread.all_copy().wait_recv()
+        value = held[:, y]
+        for j in range(1, ny):
+            value = value + spread.got[j].astype(jnp.float32)
+        return value
+
+    def multiply_far(m, first):
         products(m, lax.rem(y + ny // 2, ny))
         first.step(0, ny // 2)
+
+    def multiply_near(m, first):
         for ahead in range(1, ny):
             products(m, lax.rem(y + ny // 2 + ahead, ny))
         for ahead in range(1, ny):
@@ -522,11 +546,6 @@
     def rows_in(sums, held):
         for sub in (0, 1):
             held[sub * (wide // 2):(sub + 1) * (wide // 2), :] = sums.total(sub)
-
-    query_pair = pair_grads(0)
-    query_pair.start()
-    keep_grads(0)
-    grad_norm_scan.across_rows()
 
     def serve(h):
         query, local = after_in[h], after_in[heads + h]
@@ -536,17 +555,54 @@
         own_grads[h] += dot_nn(given, query)
         own_grads[heads + h] += dot_nn(soft.astype(jnp.bfloat16), local)
 
-    query_out.wait_recv()
-    for h in range(heads):
-        if h == heads - 1:
-            query_pair.wait_recv()
-            multiply(0, d1)
-            c1.step(0)
+    def retrieve(h):
+        mixing = mixing_of(h)
+        query = kvq[2 * heads + h].astype(jnp.float32)
+        phi = feature(query)
+        memory = memory_scan.head(h, heads)
+        retrieved = dot_nn(phi.astype(jnp.bfloat16), memory) / den[h]
+        join(h, mixing * retrieved, None)
+        grad_ret = mixing * cot[:, columns(h)].astype(jnp.float32)
+        grad_den = -jnp.sum(grad_ret * retrieved, axis=1, keepdims=True) / den[h]
+        n2_own[h] = jnp.sum(grad_den * phi, axis=0, keepdims=True)
+        grad_phi = dot_nt(grad_num[h], memory) + grad_den * norms[0, h]
+        join(h, None, grad_phi * feature_slope(query))
+
+    def attend_now(h):
+        key_out[h].wait_recv()
+        value_out[h].wait_recv()
+        attend(h)
+        stats_out[h].start()
+
+    def serve_now(h):
+        query_out[h].wait_recv()
         local_out[h].wait_recv()
         stats_out[h].wait_recv()
         serve(h)
+
+    for h in range(heads - 1):
+        attend_now(h)
+    grad_memory_scan.give_back()
+    memory_scan.finish()
+    for h in range(heads):
+        retrieve(h)
+    grad_norm_scan.start()
+    attend_now(heads - 1)
+    query_pair = pair_grads(0)
+    query_pair.start()
+    keep_grads(0)
+    grad_norm_scan.across_columns()
+    blended_out = pltpu.make_async_copy(blended, blended_ref, out_sem.at[2])
+    blended_out.start()
+    for h in range(heads - 1):
+        serve_now(h)
+    query_pair.wait_recv()
+    multiply_far(0, d1)
+    multiply_near(0, d1)
+    c1.step(0)
+    serve_now(heads - 1)
+    grad_memory_scan.finish()
     norms[1] = grad_norm_scan.result()
-    grad_memory_scan.finish()
 
     def write_back(h):
         key = kvq[h].astype(jnp.float32)
@@ -556,8 +612,8 @@
         grad_value = dot_nn(feature(key).astype(jnp.bfloat16), grad_memory)
         grads[2, h] = (own_grads[heads + h] + grad_value).astype(jnp.bfloat16)
 
+    key_pair, value_pair = pair_grads(1), pair_grads(2)
     write_back(1 - dp)
-    key_pair, value_pair = pair_grads(1), pair_grads(2)
     key_pair.start()
     value_pair.start()
     write_back(dp)
@@ -570,7 +626,8 @@
     a1.step(0)
     d1.step(1)
     value_pair.wait_recv()
-    multiply(2, b1)
+    multiply_far(2, b1)
+    multiply_near(2, b1)
     c1.step(2)
     rows_in(d1, d_sum)
     d2.step(0)
@@ -580,45 +637,51 @@
     d2.step(1)
     a1.step(2)
     columns_in(c1, c_sum)
-    c2.step(0)
+    send_parts(c2, c_sum, c2_send)
     d2.step(2)
     rows_in(b1, b_sum)
     b2.step(0)
     a1.step(3)
     d2.step(3)
     b2.step(1)
-    c2.step(1)
     columns_in(a1, a_sum)
-    a2.step(0)
+    send_parts(a2, a_sum, a2_send)
     b2.step(2)
-    a2.step(1)
-    b2.step(3)
-    places = ((c2, 0, part), (d2, part, dim), (a2, dim, 2 * dim), (b2, 2 * dim, 3 * dim))
-    for sums, left, right in places:
-        for sub in (0, 1):
-            fin[sub, :, left:right] = sums.total(sub) * scale
-    swap_out = pair_copy(fin.at[1 - dp], swap, 4)
-    swap_out.start()
 
     def put(src, m, place, slot):
         return pltpu.make_async_copy(
             src.at[:, pl.ds(m * dim, dim)], out_ref.at[m, :, columns(place)], out_sem.at[slot]
         )
 
-    own_out = [put(fin.at[dp], m, dp, 0) for m in range(3)]
-    other_out = [put(swap, m, 1 - dp, 1) for m in range(3)]
-    for copy in own_out:
-        copy.start()
+    swaps = [
+        pair_copy(fin.at[1 - dp, :, pl.ds(m * dim, dim)], swap.at[:, pl.ds(m * dim, dim)], 4 + m) for m in range(3)
+    ]
+
+    def hand_over(m):
+        swaps[m].start()
+        put(fin.at[dp], m, dp, 0).start()
+
+    fin[:, :, 0:part] = direct_total(c2, c_sum) * scale
+    for sub in (0, 1):
+        fin[sub, :, part:dim] = d2.total(sub) * scale
+    hand_over(0)
+    b2.step(3)
+    fin[:, :, dim:2 * dim] = direct_total(a2, a_sum) * scale
+    hand_over(1)
+    for sub in (0, 1):
+        fin[sub, :, 2 * dim:3 * dim] = b2.total(sub) * scale
+    hand_over(2)
     for sent in (
         a1, b1, c1, d1, a2, b2, c2, d2, norm_scan, grad_norm_scan, memory_scan, grad_memory_scan,
     ):
         sent.drain()
-    for copy in (*key_out, *value_out, *local_out, query_out, *stats_out, x_out, query_pair, key_pair, value_pair):
+    for copy in (*key_out, *value_out, *local_out, *query_out, *stats_out, x_out, query_pair, key_pair, value_pair):
         copy.wait_send()
-    swap_out.wait_recv()
-    for copy in other_out:
-        copy.start()
-    swap_out.wait_send()
+    for m in range(3):
+        swaps[m].wait_recv()
+        put(swap, m, 1 - dp, 1).start()
+    for m in range(3):
+        swaps[m].wait_send()
     blended_out.wait()
     for slot in (0, 1):
         pltpu.make_async_copy(fin.at[slot], swap, out_sem.at[slot]).wait()
@@ -659,16 +722,17 @@
             real(heads, tokens, tokens), real(heads, tokens, tokens), wire(heads, tokens, dim),
             wire(heads, tokens, dim), real(heads, tokens, 1), real(heads, 8, tokens), real(heads, 8, tokens),
             wire(3, heads, tokens, dim), wire(3, 2 * tokens, dim),
-            *vectors, *vectors, real(2, heads, 1, dim), *scan, *scan,
+            *vectors, real(heads, 1, dim), real(ny, heads, 1, dim), real(2, heads, 1, dim), real(nz, 2, heads, 1, dim),
+            real(2, heads, 1, dim), *scan, *scan,
             real(3, ny, wide, dim), real(2, ny, rows, dim), real(wide, dim), real(2, ny, rows, dim // 2), real(wide, dim // 2),
             real(2, rows, 3 * dim), real(rows, 3 * dim),
             wire(*a1, dim), wire(*a1, dim), wire(*b1, dim), wire(*b1, dim),
             wire(*a1, dim // 2), wire(*a1, dim // 2), wire(*b1, dim // 2), wire(*b1, dim // 2),
-            wire(ys, rows, dim), wire(ys, rows, dim), wire(zs, rows, dim), wire(zs, rows, dim),
-            wire(ys, rows, dim // 2), wire(ys, rows, dim // 2), wire(zs, rows, dim // 2), wire(zs, rows, dim // 2),
-            dma(2 + 3 * heads), dma(2, 4 * heads + 1), dma(2, 5), dma(2, 2), dma(2, 2),
+            wire(ny, 2, rows, dim), wire(ny, 2, rows, dim), wire(zs, rows, dim), wire(zs, rows, dim),
+            wire(ny, 2, rows, dim // 2), wire(ny, 2, rows, dim // 2), wire(zs, rows, dim // 2), wire(zs, rows, dim // 2),
+            dma(2 + 3 * heads), dma(2, 5 * heads), dma(2, 7), dma(2, 2), dma(2, 2),
             dma(2, 2), dma(2, 2), dma(2, 2),
-            dma(4, zs), dma(4, ys), dma(8), dma(3),
+            dma(4, zs), dma(2, ys), dma(8), dma(2, 2), dma(3),
         ],
         compiler_params=pltpu.CompilerParams(
             collective_id=1, has_side_effects=True, vmem_limit_bytes=63 * 1024 * 1024
@@ -677,17 +741,18 @@
 
 
 def hand_on_kernel(a_ref, b_ref, a_out, b_out, a_held, b_held, sem):
-    steps = [
-        (pltpu.make_async_copy(src, held, sem.at[0, i]), pltpu.make_async_copy(held, dst, sem.at[1, i]))
-        for i, (src, held, dst) in enumerate(((a_ref, a_held, a_out), (b_ref, b_held, b_out)))
-    ]
-    for first, _ in steps:
-        first.start()
-    for first, second in steps:
-        first.wait()
-        second.start()
-    for _, second in steps:
-        second.wait()
+    size = a_ref.shape[0] // PIECES
+    whole = [(b_ref.at[m], b_held.at[m], b_out.at[m]) for m in range(b_ref.shape[0])]
+    whole += [tuple(ref.at[pl.ds(i * size, size)] for ref in (a_ref, a_held, a_out)) for i in range(PIECES)]
+    reads = [pltpu.make_async_copy(src, held, sem.at[0, i]) for i, (src, held, _) in enumerate(whole)]
+    writes = [pltpu.make_async_copy(held, dst, sem.at[1, i]) for i, (_, held, dst) in enumerate(whole)]
+    for read in reads:
+        read.start()
+    for read, write in zip(reads, writes):
+        read.wait()
+        write.start()
+    for write in writes:
+        write.wait()
 
 
 def hand_on(a, b):
@@ -697,7 +762,8 @@
         out_shape=tuple(jax.ShapeDtypeStruct(v.shape, v.dtype) for v in (a, b)),
         in_specs=[anywhere] * 2,
         out_specs=(anywhere,) * 2,
-        scratch_shapes=[pltpu.VMEM(v.shape, v.dtype) for v in (a, b)] + [pltpu.SemaphoreType.DMA((2, 2))],
+        scratch_shapes=[pltpu.VMEM(v.shape, v.dtype) for v in (a, b)]
+        + [pltpu.SemaphoreType.DMA((2, PIECES + b.shape[0]))],
     )(a, b)
 
 

time: 96.5 us -> 96.7 us (level)
  no operation moved by 1% of the time
where the time goes in v6:
time: 96.7 us; the launch traced here: 96.6 us
  Pallas kernels  95.8 us (99%)
    pallas_call x1, Pallas kernels, layer(): pl.pallas_call(functools.partial(layer_kernel, scale), out_shape=(jax.Sha...  93.9 us
    pallas_call x1, Pallas kernels, hand_on(): pl.pallas_call(hand_on_kernel, out_shape=tuple((jax.ShapeDtypeStruct(v.sh...  1.94 us

profile of v6, /device:TPU:1, one launch (start us, length us, event | category | flops | bytes accessed | tf_op | source)
XLA Modules:
  0.0 96.6 jit_solution(6222867781200933377)
XLA Ops:
  0.6 93.9 %shard_map.77 = (bf16[384,512]{1,0:T(8,128)(2,1)}, f32[3,48,512]{2,1,0:T(8,128)}) custom-call(bf16[384,3072]{1,0:T(8,128)(2,1)} %bitcast.4, bf16[3072,512]{1,0:T(8,128)(2,1)} %wq_ref.1, bf16[3072,512]{1,0:T(8,128)(2,1)} %wk_ref.1, bf16[3072,512]{1,0:T(8,128)(2,1)} %wv_ref.1, f32[2]{0:T(128)} %gate_ref.1, bf16[384,512]{1,0:T(8,128)(2,1)} %bitcast.5), custom_call_target="tpu_custom_call" | custom-call | tf_op jit(solution)/shard_map/pallas_call | solution.py:710
  94.5 1.9 %shard_map.78 = (bf16[384,512]{1,0:T(8,128)(2,1)}, f32[3,48,512]{2,1,0:T(8,128)}) custom-call(bf16[384,512]{1,0:T(8,128)(2,1)} %get-tuple-element.6.a_ref, f32[3,48,512]{2,1,0:T(8,128)} %get-tuple-element.7.b_ref), custom_call_target="tpu_custom_call" | custom-call | tf_op jit(solution)/shard_map/pallas_call | solution.py:760

commit v7 on v6

--- a/solution.py
+++ b/solution.py
@@ -533,15 +533,14 @@
             value = value + spread.got[j].astype(jnp.float32)
         return value
 
-    def multiply_far(m, first):
-        products(m, lax.rem(y + ny // 2, ny))
-        first.step(0, ny // 2)
-
-    def multiply_near(m, first):
-        for ahead in range(1, ny):
-            products(m, lax.rem(y + ny // 2 + ahead, ny))
-        for ahead in range(1, ny):
-            first.step(0, ny // 2 + ahead)
+    def multiply(m):
+        for k in range(ny):
+            products(m, k)
+
+    def first_hop(sums):
+        for ahead in range(ny):
+            sums.step(0, ny // 2 + ahead)
+
 
     def rows_in(sums, held):
         for sub in (0, 1):
@@ -597,37 +596,39 @@
     for h in range(heads - 1):
         serve_now(h)
     query_pair.wait_recv()
-    multiply_far(0, d1)
-    multiply_near(0, d1)
+    multiply(0)
     c1.step(0)
+    first_hop(d1)
     serve_now(heads - 1)
     grad_memory_scan.finish()
     norms[1] = grad_norm_scan.result()
 
-    def write_back(h):
-        key = kvq[h].astype(jnp.float32)
-        grad_memory = grad_memory_scan.head(h, heads)
-        grad_phi = dot_nt(kvq[heads + h], grad_memory) + norms[1, h]
-        grads[1, h] = (own_grads[h] + grad_phi * feature_slope(key)).astype(jnp.bfloat16)
-        grad_value = dot_nn(feature(key).astype(jnp.bfloat16), grad_memory)
-        grads[2, h] = (own_grads[heads + h] + grad_value).astype(jnp.bfloat16)
+    def write_key(h):
+        grad_phi = dot_nt(kvq[heads + h], grad_memory_scan.head(h, heads)) + norms[1, h]
+        slope = feature_slope(kvq[h].astype(jnp.float32))
+        grads[1, h] = (own_grads[h] + grad_phi * slope).astype(jnp.bfloat16)
+
+    def write_value(h):
+        phi = feature(kvq[h].astype(jnp.float32)).astype(jnp.bfloat16)
+        grads[2, h] = (own_grads[heads + h] + dot_nn(phi, grad_memory_scan.head(h, heads))).astype(jnp.bfloat16)
 
     key_pair, value_pair = pair_grads(1), pair_grads(2)
-    write_back(1 - dp)
+    write_key(1 - dp)
     key_pair.start()
+    write_key(dp)
+    write_value(1 - dp)
     value_pair.start()
-    write_back(dp)
+    write_value(dp)
     keep_grads(1)
     keep_grads(2)
+    c1.step(1)
+    d1.step(1)
     key_pair.wait_recv()
-    for k in range(ny):
-        products(1, k)
-    c1.step(1)
+    multiply(1)
     a1.step(0)
-    d1.step(1)
     value_pair.wait_recv()
-    multiply_far(2, b1)
-    multiply_near(2, b1)
+    multiply(2)
+    first_hop(b1)
     c1.step(2)
     rows_in(d1, d_sum)
     d2.step(0)

time: 96.7 us -> 95.4 us (0.987)
  Pallas kernels: 95.8 us -> 94.5 us
    pallas_call x1, Pallas kernels: 93.9 us -> 92.5 us  [layer(): pl.pallas_call(functools.partial(layer_kernel, scale), out_shape=(jax.Sha...]
where the time goes in v7:
time: 95.4 us; the launch traced here: 95.3 us
  Pallas kernels  94.5 us (99%)
    pallas_call x1, Pallas kernels, layer(): pl.pallas_call(functools.partial(layer_kernel, scale), out_shape=(jax.Sha...  92.5 us
    pallas_call x1, Pallas kernels, hand_on(): pl.pallas_call(hand_on_kernel, out_shape=tuple((jax.ShapeDtypeStruct(v.sh...  1.94 us

profile of v7, /device:TPU:1, one launch (start us, length us, event | category | flops | bytes accessed | tf_op | source)
XLA Modules:
  0.0 95.3 jit_solution(6727838853501294389)
XLA Ops:
  0.6 92.5 %shard_map.77 = (bf16[384,512]{1,0:T(8,128)(2,1)}, f32[3,48,512]{2,1,0:T(8,128)}) custom-call(bf16[384,3072]{1,0:T(8,128)(2,1)} %bitcast.4, bf16[3072,512]{1,0:T(8,128)(2,1)} %wq_ref.1, bf16[3072,512]{1,0:T(8,128)(2,1)} %wk_ref.1, bf16[3072,512]{1,0:T(8,128)(2,1)} %wv_ref.1, f32[2]{0:T(128)} %gate_ref.1, bf16[384,512]{1,0:T(8,128)(2,1)} %bitcast.5), custom_call_target="tpu_custom_call" | custom-call | tf_op jit(solution)/shard_map/pallas_call | solution.py:711
  93.2 1.9 %shard_map.78 = (bf16[384,512]{1,0:T(8,128)(2,1)}, f32[3,48,512]{2,1,0:T(8,128)}) custom-call(bf16[384,512]{1,0:T(8,128)(2,1)} %get-tuple-element.6.a_ref, f32[3,48,512]{2,1,0:T(8,128)} %get-tuple-element.7.b_ref), custom_call_target="tpu_custom_call" | custom-call | tf_op jit(solution)/shard_map/pallas_call | solution.py:761

commit v8 on v7

--- a/solution.py
+++ b/solution.py
@@ -630,24 +630,24 @@
     multiply(2)
     first_hop(b1)
     c1.step(2)
+    a1.step(1)
     rows_in(d1, d_sum)
-    d2.step(0)
-    a1.step(1)
     b1.step(1)
     c1.step(3)
-    d2.step(1)
+    d2.step(0)
     a1.step(2)
     columns_in(c1, c_sum)
     send_parts(c2, c_sum, c2_send)
-    d2.step(2)
+    d2.step(1)
     rows_in(b1, b_sum)
     b2.step(0)
     a1.step(3)
-    d2.step(3)
+    d2.step(2)
     b2.step(1)
     columns_in(a1, a_sum)
     send_parts(a2, a_sum, a2_send)
     b2.step(2)
+    d2.step(3)
 
     def put(src, m, place, slot):
         return pltpu.make_async_copy(
@@ -662,11 +662,11 @@
         swaps[m].start()
         put(fin.at[dp], m, dp, 0).start()
 
+    b2.step(3)
     fin[:, :, 0:part] = direct_total(c2, c_sum) * scale
     for sub in (0, 1):
         fin[sub, :, part:dim] = d2.total(sub) * scale
     hand_over(0)
-    b2.step(3)
     fin[:, :, dim:2 * dim] = direct_total(a2, a_sum) * scale
     hand_over(1)
     for sub in (0, 1):

time: 95.4 us -> 95.1 us (level)
  no operation moved by 1% of the time
where the time goes in v8:
time: 95.1 us; the launch traced here: 94.9 us
  Pallas kernels  94.1 us (99%)
    pallas_call x1, Pallas kernels, layer(): pl.pallas_call(functools.partial(layer_kernel, scale), out_shape=(jax.Sha...  92.2 us
    pallas_call x1, Pallas kernels, hand_on(): pl.pallas_call(hand_on_kernel, out_shape=tuple((jax.ShapeDtypeStruct(v.sh...  1.94 us

profile of v8, /device:TPU:1, one launch (start us, length us, event | category | flops | bytes accessed | tf_op | source)
XLA Modules:
  0.0 94.9 jit_solution(14239580743875173940)
XLA Ops:
  0.6 92.2 %shard_map.77 = (bf16[384,512]{1,0:T(8,128)(2,1)}, f32[3,48,512]{2,1,0:T(8,128)}) custom-call(bf16[384,3072]{1,0:T(8,128)(2,1)} %bitcast.4, bf16[3072,512]{1,0:T(8,128)(2,1)} %wq_ref.1, bf16[3072,512]{1,0:T(8,128)(2,1)} %wk_ref.1, bf16[3072,512]{1,0:T(8,128)(2,1)} %wv_ref.1, f32[2]{0:T(128)} %gate_ref.1, bf16[384,512]{1,0:T(8,128)(2,1)} %bitcast.5), custom_call_target="tpu_custom_call" | custom-call | tf_op jit(solution)/shard_map/pallas_call | solution.py:711
  92.8 1.9 %shard_map.78 = (bf16[384,512]{1,0:T(8,128)(2,1)}, f32[3,48,512]{2,1,0:T(8,128)}) custom-call(bf16[384,512]{1,0:T(8,128)(2,1)} %get-tuple-element.6.a_ref, f32[3,48,512]{2,1,0:T(8,128)} %get-tuple-element.7.b_ref), custom_call_target="tpu_custom_call" | custom-call | tf_op jit(solution)/shard_map/pallas_call | solution.py:761
